TPU v7x, 32 devices: a whole 2x2x4 slice. The times are simulated.
32 devices in a mesh: sx: 4 (over y, core), sy: 8 (over z, x).
Axes of the slice: x: 2, y: 2, z: 4, core: 2. Of those that a mesh axis runs over, the one named last changes fastest.
Arguments:
- basis: bfloat16 [4, 8, 8192, 512], P('sx', 'sy'), may hold values from -0.06629126 to 0.06629126
- diag_weight: float32 [4, 8, 8192], P('sx', 'sy'), may hold values from 0.5 to 4
- correlation_weight: float32 [4, 8, 2, 2048], P('sx', 'sy'), may hold values from 0.05 to 0.4
- tile_ids: int32 [4, 8, 4, 16], P('sx', 'sy'), may hold values from 0 to 63
- pair_live: int32 [4, 8, 2], replicated, may hold values 0 or 1
- loads: float32 [4, 8, 512, 256], P('sx', 'sy'), may hold values from -6 to 6
- load_count: int32 [4, 8], P('sx', 'sy'), may hold values from 1 to 256
Outputs:
- coeffs: float32 [4, 8, 512, 256], P('sx', 'sy')
Inputs may be any that keep to these rules, and one draw needn't show every extreme that they name: Entries of pair_live for pairs beyond the grid's last column (index 0) or last row (index 1) are read by no step.
All inputs are finite; a program needn't handle non-finite values.
Results may differ from a plain program's by a relative error of at most 0.0015.
Values may be sent and summed in bfloat16 or wider, within the bound.
A program may use at most 128 MiB of HBM per device.

v0:
```python
import jax
import jax.numpy as jnp
from jax import lax
from jax.sharding import PartitionSpec as P

TILE = 128
ITERS = 3


damping = 0.8


def passed_along(block, axis, distance):
    devices = range(lax.axis_size(axis))
    route = [(i - distance, i) for i in devices if i - distance in devices]
    return lax.ppermute(block, axis, route)


def shortened(x):
    return jax.tree.map(lambda a: a.astype(jnp.bfloat16) if a.dtype == jnp.float32 else a, x)


def extended(x, sides, width):
    for axis, dim in sides:
        peers, length = (lax.axis_size(axis), x.shape[dim])
        up = [(i, (i + 1) % peers) for i in range(peers - 1)]
        down = [(j, i) for i, j in up]
        last = lax.slice_in_dim(x, length - width, length, axis=dim)
        initial = lax.slice_in_dim(x, 0, width, axis=dim)
        before = lax.ppermute(last, axis, up)
        after = lax.ppermute(initial, axis, down)
        x = jnp.concatenate([before, x, after], axis=dim)
    return x


def stencil(rows_in, weight):
    values = rows_in.astype(jnp.float32)
    zero_row = jnp.zeros_like(values[:1])
    before = jnp.concatenate([zero_row, values[:-1]], axis=0)
    after = jnp.concatenate([values[1:], zero_row], axis=0)
    return weight[:, None] * (2.5 * values - before - after)


def interface(tiled, tile_list):
    return jnp.take(tiled, tile_list, axis=0).reshape(-1, tiled.shape[2])


def contract(left_rows, right_rows):
    return lax.dot_general(
        left_rows, right_rows, (((0,), (0,)), ((), ())), preferred_element_type=jnp.float32
    )


def apply_block(block, vector):
    return jnp.dot(
        block, vector, precision=lax.Precision.HIGHEST, preferred_element_type=jnp.float32
    )


def mirror_block(block, vector):
    return lax.dot_general(
        block,
        vector,
        (((0,), (0,)), ((), ())),
        precision=lax.Precision.HIGHEST,
        preferred_element_type=jnp.float32,
    )


def masked_block(live, left_rows, right_rows):
    width = left_rows.shape[1]
    return lax.cond(
        live,
        lambda: contract(left_rows, right_rows),
        lambda: jnp.zeros((width, width), jnp.float32),
    )


def on_device(basis, diag_weight, correlation_weight, tile_ids, pair_live, loads, load_count):
    local_basis = basis[0, 0]
    width = local_basis.shape[1]
    tiled = local_basis.reshape(-1, TILE, width)
    row_at = lax.axis_index("sx")
    col_at = lax.axis_index("sy")
    row_count = lax.axis_size("sx")
    col_count = lax.axis_size("sy")
    live_east = jnp.logical_and(pair_live[row_at, col_at, 0] > 0, col_at < col_count - 1)
    live_south = jnp.logical_and(pair_live[row_at, col_at, 1] > 0, row_at < row_count - 1)
    image_west = stencil(interface(tiled, tile_ids[0, 0, 0]), correlation_weight[0, 0, 0]).astype(
        jnp.bfloat16
    )
    image_north = stencil(interface(tiled, tile_ids[0, 0, 2]), correlation_weight[0, 0, 1]).astype(
        jnp.bfloat16
    )
    east_rows = interface(tiled, tile_ids[0, 0, 1])
    south_rows = interface(tiled, tile_ids[0, 0, 3])
    from_east = passed_along(image_west, "sy", -1)
    from_south = passed_along(image_north, "sx", -1)
    weighted = (diag_weight[0, 0][:, None] * local_basis.astype(jnp.float32)).astype(jnp.bfloat16)
    diagonal_block = contract(local_basis, weighted)
    block_east = masked_block(live_east, east_rows, from_east)
    block_south = masked_block(live_south, south_rows, from_south)
    live_west = jnp.logical_and(pair_live[row_at, jnp.maximum(col_at - 1, 0), 0] > 0, col_at > 0)
    live_north = jnp.logical_and(pair_live[jnp.maximum(row_at - 1, 0), col_at, 1] > 0, row_at > 0)
    from_west = passed_along(east_rows, "sy", 1)
    from_north = passed_along(south_rows, "sx", 1)
    block_west = masked_block(live_west, from_west, image_west)
    block_north = masked_block(live_north, from_north, image_north)
    factor = jnp.linalg.cholesky(diagonal_block)
    columns = loads.shape[3]
    live_cols = (jnp.arange(columns, dtype=jnp.int32) < load_count[0, 0]).astype(jnp.float32)
    rhs = loads[0, 0] * live_cols[None, :]
    coeffs = damping * jax.scipy.linalg.cho_solve((factor, True), rhs)
    for sweep in range(1, ITERS):
        nearby = extended(shortened(coeffs[None, None]), (("sx", 0), ("sy", 1)), 1)
        residual = (
            rhs
            - apply_block(diagonal_block, coeffs)
            - apply_block(block_east, nearby[1, 2])
            - apply_block(block_south, nearby[2, 1])
        )
        residual = (
            residual
            - mirror_block(block_west, nearby[1, 0])
            - mirror_block(block_north, nearby[0, 1])
        )
        coeffs = coeffs + damping * jax.scipy.linalg.cho_solve((factor, True), residual)
    return coeffs[None, None]


def solution(mesh):
    return jax.shard_map(
        on_device,
        mesh=mesh,
        in_specs=(
            P("sx", "sy", None, None),
            P("sx", "sy", None),
            P("sx", "sy", None, None),
            P("sx", "sy", None, None),
            P(),
            P("sx", "sy", None, None),
            P("sx", "sy"),
        ),
        out_specs=P("sx", "sy", None, None),
        check_vma=False,
    )
```

profile of v0, /device:TPU:1, one launch (start us, length us, event | category | flops | bytes accessed | tf_op | source)
XLA Modules:
  0.0 320.3 jit_solution(9027148926387089196)
XLA Ops:
  0.9 5.4 %gather_fusion.3 = bf16[16,128,512]{2,1,0:T(8,128)(2,1)} fusion(bf16[64,128,512]{2,1,0:T(8,128)(2,1)} %bitcast.190, s32[1024]{0:T(1024)S(1)} %pad_clamp_fusion), kind=kCustom, calls=%fused_computation.3.clone | custom fusion | bytes 4194368 | tf_op jit(solution)/shard_map/jit(_take)/gather | solution.py:45
  6.2 1.8 broadcast_select_fusion
  9.8 2.6 multiply_convert_fusion.1
  12.4 1.9 collective-permute-start.4
  14.4 4.1 %gather_fusion = bf16[16,128,512]{2,1,0:T(8,128)(2,1)S(1)} fusion(bf16[64,128,512]{2,1,0:T(8,128)(2,1)} %bitcast.191, s32[1024]{0:T(1024)S(1)} %pad_clamp_fusion.3), kind=kCustom, calls=%fused_computation.clone | custom fusion | bytes 4194368 | tf_op jit(solution)/shard_map/jit(_take)/gather | solution.py:45
  20.0 5.9 %collective-permute-start.5 = (bf16[2048,512]{1,0:T(8,128)(2,1)}, bf16[2048,512]{1,0:T(8,128)(2,1)}, u32[]{:S(2)}, u32[]{:S(2)}) collective-permute-start(bf16[2048,512]{1,0:T(8,128)(2,1)} %bitcast.20), channel_id=1, source_target_pairs={{0,1},{1,2},{2,3},{3,4},{4,5},{5,6},{6,7},{8,9},{9,10},{10,11},{11... | collective-permute-start | bytes 6291464 | tf_op jit(solution)/shard_map/ppermute | solution.py:16
  25.9 4.1 %gather_fusion.2 = bf16[16,128,512]{2,1,0:T(8,128)(2,1)S(1)} fusion(bf16[64,128,512]{2,1,0:T(8,128)(2,1)} %bitcast.192, s32[1024]{0:T(1024)S(1)} %pad_clamp_fusion.1), kind=kCustom, calls=%fused_computation.2.clone | custom fusion | bytes 4194368 | tf_op jit(solution)/shard_map/jit(_take)/gather | solution.py:45
  31.6 3.3 %collective-permute-start.7 = (bf16[2048,512]{1,0:T(8,128)(2,1)}, bf16[2048,512]{1,0:T(8,128)(2,1)}, u32[]{:S(2)}, u32[]{:S(2)}) collective-permute-start(bf16[2048,512]{1,0:T(8,128)(2,1)} %bitcast.29), channel_id=1, source_target_pairs={{0,8},{8,16},{16,24},{1,9},{9,17},{17,25},{2,10},{10,18},{18,26},{... | collective-permute-start | bytes 6291464 | tf_op jit(solution)/shard_map/ppermute | solution.py:16
  35.0 5.4 %gather_fusion.1 = bf16[16,128,512]{2,1,0:T(8,128)(2,1)} fusion(bf16[64,128,512]{2,1,0:T(8,128)(2,1)} %bitcast.193, s32[1024]{0:T(1024)S(1)} %pad_clamp_fusion.2), kind=kCustom, calls=%fused_computation.1.clone | custom fusion | bytes 4194368 | tf_op jit(solution)/shard_map/jit(_take)/gather | solution.py:45
  40.3 1.8 broadcast_select_fusion.2
  43.9 2.6 multiply_convert_fusion.2
  48.0 10.4 %fusion.1 = f32[512,512]{1,0:T(8,128)S(1)} fusion(bf16[1,1,8192,512]{3,2,1,0:T(8,128)(2,1)} %param.19, f32[8192]{0:T(1024)S(1)} %bitcast.196), kind=kOutput, calls=%fused_computation.8 | convolution fusion | flops 4307550208 | bytes 9469952 | tf_op jit(solution)/shard_map/dot_general | solution.py:49
  60.1 11.7 %cholesky.104 = f32[128,128]{1,0:T(8,128)S(1)} custom-call(f32[128,128]{1,0:T(8,128)S(1)} %cholesky.266), custom_call_target="Cholesky" | custom-call | tf_op jit(solution)/shard_map/jit(cholesky)/cholesky | solution.py:109
  71.8 9.8 %custom-call.32 = f32[1,128,128]{1,2,0:T(8,128)S(1)} custom-call(f32[1,128,128]{2,1,0:T(8,128)S(1)} %get-tuple-element.99), custom_call_target="InvertDiagBlocksLowerTriangular" | custom-call | tf_op jit(solution)/shard_map/jit(cholesky)/cholesky | solution.py:109
  84.3 12.1 %cholesky.217 = f32[128,128]{1,0:T(8,128)S(1)} custom-call(f32[128,128]{1,0:T(8,128)S(1)} %cholesky.270), custom_call_target="Cholesky" | custom-call | tf_op jit(solution)/shard_map/jit(cholesky)/cholesky | solution.py:109
  96.4 9.8 %custom-call.33 = f32[1,128,128]{1,2,0:T(8,128)S(1)} custom-call(f32[1,128,128]{2,1,0:T(8,128)S(1)} %get-tuple-element.96), custom_call_target="InvertDiagBlocksLowerTriangular" | custom-call | tf_op jit(solution)/shard_map/jit(cholesky)/cholesky | solution.py:109
  107.8 11.7 %cholesky.238 = f32[128,128]{1,0:T(8,128)S(1)} custom-call(f32[128,128]{1,0:T(8,128)S(1)} %cholesky.275), custom_call_target="Cholesky" | custom-call | tf_op jit(solution)/shard_map/jit(cholesky)/cholesky | solution.py:109
  120.2 9.8 %custom-call.34 = f32[1,128,128]{1,2,0:T(8,128)S(1)} custom-call(f32[1,128,128]{2,1,0:T(8,128)S(1)} %get-tuple-element.93), custom_call_target="InvertDiagBlocksLowerTriangular" | custom-call | tf_op jit(solution)/shard_map/jit(cholesky)/cholesky | solution.py:109
  131.6 11.7 %cholesky.255 = f32[128,128]{1,0:T(8,128)S(1)} custom-call(f32[128,128]{1,0:T(8,128)S(1)} %convolution_subtract_fusion.18), custom_call_target="Cholesky" | custom-call | tf_op jit(solution)/shard_map/jit(cholesky)/cholesky | solution.py:109
  147.4 10.7 %while.6 = (s32[]{:T(128)}, f32[512,512]{1,0:T(8,128)S(1)}, s32[4,2]{0,1:T(2,128)S(1)}, f32[4,128,128]{2,1,0:T(8,128)}, s32[]{:T(128)}) while((s32[]{:T(128)}, f32[512,512]{1,0:T(8,128)S(1)}, s32[4,2]{0,1:T(2,128)S(1)}, f32[4,128,128]{2,1,0:T(8,128)}, s32[]{:T(128)}) %tuple.85), condition=%wide.while_cond, body=%wide.while_body.sunk | while | flops 2 | bytes 132705 | solution.py:113
  148.1 2.0 bitcast_dynamic-update-slice_fusion.2
  150.8 2.0 bitcast_dynamic-update-slice_fusion.2
  153.5 2.0 bitcast_dynamic-update-slice_fusion.2
  156.1 2.0 bitcast_dynamic-update-slice_fusion.2
  158.1 40.1 %custom-call.37 = f32[4,128,128]{1,2,0:T(8,128)S(1)} custom-call(f32[4,128,128]{2,1,0:T(8,128)} %get-tuple-element.63), custom_call_target="InvertDiagBlocksLowerTriangular" | custom-call | tf_op jit(solution)/shard_map/jit(_cho_solve)/triangular_solve | solution.py:113
  205.3 2.4 collective-permute-start.2
  207.7 5.6 %collective-permute-done.2 = bf16[1,1,512,256]{3,2,1,0:T(8,128)(2,1)} collective-permute-done((bf16[1,1,512,256]{3,2,1,0:T(8,128)(2,1)}, bf16[1,1,512,256]{3,2,1,0:T(8,128)(2,1)}, u32[]{:S(2)}, u32[]{:S(2)}) %collective-permute-start.2) | collective-permute-done | bytes 262176 | tf_op jit(solution)/shard_map/ppermute | solution.py:31
  213.3 1.9 collective-permute-start.1
  218.8 2.1 pad_maximum_fusion
  220.9 5.1 %collective-permute-start.6 = (bf16[3,1,512,256]{3,2,1,0:T(8,128)(2,1)}, bf16[3,1,512,256]{3,2,1,0:T(8,128)(2,1)}, u32[]{:S(2)}, u32[]{:S(2)}) collective-permute-start(bf16[3,1,512,256]{3,2,1,0:T(8,128)(2,1)} %pad_maximum_fusion), channel_id=1, source_target_pairs={{0,1},{1,2},{2,3},{3,4},{4,5},{5,6},{6,7},{8,9},{9,10},{10,11},{11... | collective-permute-start | bytes 2359304 | tf_op jit(solution)/shard_map/ppermute | solution.py:30
  226.1 2.6 convolution_subtract_fusion.3
  230.0 3.5 %conditional.5 = (f32[512,512]{1,0:T(8,128)S(1)}) conditional(s32[]{:T(128)} %convert_element_type.69, () %tuple.33, (bf16[2048,512]{1,0:T(8,128)(2,1)}, bf16[2048,512]{1,0:T(8,128)(2,1)}) %tuple.34), branch_computations={%region_10.13_spmd, %region_11.14_spmd} | conditional | flops 1073741824 | bytes 5242888 | solution.py:72
  230.0 3.5 %fusion.155 = f32[512,512]{1,0:T(8,128)S(1)} fusion(bf16[2048,512]{1,0:T(8,128)(2,1)} %get-tuple-element.32, bf16[2048,512]{1,0:T(8,128)(2,1)} %get-tuple-element.36), kind=kOutput, calls=%fused_computation.249 | convolution fusion | flops 1073741824 | bytes 5242880 | tf_op jit(solution)/shard_map/cond/branch_1_fun/dot_general | solution.py:49
  234.7 4.5 %conditional.7 = (f32[512,512]{1,0:T(8,128)}) conditional(s32[]{:T(128)} %convert_element_type.74, () %tuple.37, (bf16[2048,512]{1,0:T(8,128)(2,1)}, bf16[2048,512]{1,0:T(8,128)(2,1)}) %tuple.38), branch_computations={%region_14.17_spmd, %region_15.18_spmd} | conditional | flops 1073741824 | bytes 5242888 | solution.py:72
  234.7 4.5 %fusion.157 = f32[512,512]{1,0:T(8,128)} fusion(bf16[2048,512]{1,0:T(8,128)(2,1)} %get-tuple-element.41, bf16[2048,512]{1,0:T(8,128)(2,1)} %get-tuple-element.42), kind=kOutput, calls=%fused_computation.251 | convolution fusion | flops 1073741824 | bytes 5242880 | tf_op jit(solution)/shard_map/cond/branch_1_fun/dot_general | solution.py:49
  239.2 4.5 %conditional.4 = (f32[512,512]{1,0:T(8,128)}) conditional(s32[]{:T(128)} %convert_element_type.63, () %tuple.31, (bf16[2048,512]{1,0:T(8,128)(2,1)}, bf16[2048,512]{1,0:T(8,128)(2,1)}) %tuple.32), branch_computations={%region_8.0_spmd, %region_9.12_spmd} | conditional | flops 1073741824 | bytes 5242888 | solution.py:72
  239.2 4.5 %fusion.154 = f32[512,512]{1,0:T(8,128)} fusion(bf16[2048,512]{1,0:T(8,128)(2,1)} %get-tuple-element.30, bf16[2048,512]{1,0:T(8,128)(2,1)} %get-tuple-element.31), kind=kOutput, calls=%fused_computation.248 | convolution fusion | flops 1073741824 | bytes 5242880 | tf_op jit(solution)/shard_map/cond/branch_1_fun/dot_general | solution.py:49
  243.7 1.7 fusion.76
  245.4 2.4 fusion.74
  247.7 10.4 %collective-permute-done.6 = bf16[3,1,512,256]{3,2,1,0:T(8,128)(2,1)} collective-permute-done((bf16[3,1,512,256]{3,2,1,0:T(8,128)(2,1)}, bf16[3,1,512,256]{3,2,1,0:T(8,128)(2,1)}, u32[]{:S(2)}, u32[]{:S(2)}) %collective-permute-start.6) | collective-permute-done | bytes 786464 | tf_op jit(solution)/shard_map/ppermute | solution.py:30
  258.1 2.0 fusion.48
  260.1 1.6 fusion.10
  266.5 3.9 %collective-permute-start.9 = (bf16[1,1,512,256]{3,2,1,0:T(8,128)(2,1)S(1)}, bf16[1,1,512,256]{3,2,1,0:T(8,128)(2,1)S(1)}, u32[]{:S(2)}, u32[]{:S(2)}) collective-permute-start(bf16[1,1,512,256]{3,2,1,0:T(8,128)(2,1)S(1)} %get-tuple-element.74), channel_id=1, source_target_pairs={{8,0},{16,8},{24,16},{9,1},{17,9},{25,17},{10,2},{18,10},{26,18},{... | collective-permute-start | bytes 786440 | tf_op jit(solution)/shard_map/ppermute | solution.py:31
  270.4 1.9 collective-permute-start.8
  272.3 1.8 collective-permute-done.9
  275.7 4.1 %collective-permute-start.11 = (bf16[3,1,512,256]{3,2,1,0:T(8,128)(2,1)S(1)}, bf16[3,1,512,256]{3,2,1,0:T(8,128)(2,1)S(1)}, u32[]{:S(2)}, u32[]{:S(2)}) collective-permute-start(bf16[3,1,512,256]{3,2,1,0:T(8,128)(2,1)S(1)} %pad_maximum_fusion.1), channel_id=1, source_target_pairs={{0,1},{1,2},{2,3},{3,4},{4,5},{5,6},{6,7},{8,9},{9,10},{10,11},{11... | collective-permute-start | bytes 2359304 | tf_op jit(solution)/shard_map/ppermute | solution.py:30
  279.9 1.8 convolution_subtract_fusion.1
  284.7 28.1 %collective-permute-done.11 = bf16[3,1,512,256]{3,2,1,0:T(8,128)(2,1)S(1)} collective-permute-done((bf16[3,1,512,256]{3,2,1,0:T(8,128)(2,1)S(1)}, bf16[3,1,512,256]{3,2,1,0:T(8,128)(2,1)S(1)}, u32[]{:S(2)}, u32[]{:S(2)}) %collective-permute-start.11) | collective-permute-done | bytes 786464 | tf_op jit(solution)/shard_map/ppermute | solution.py:30
  (141 shorter events, 48.1 us)
Async XLA Ops:
  8.8 1.0 copy-start.13
  12.4 216.3 %collective-permute-start.4 = (bf16[2048,512]{1,0:T(8,128)(2,1)}, bf16[2048,512]{1,0:T(8,128)(2,1)}, u32[]{:S(2)}, u32[]{:S(2)}) collective-permute-start(bf16[2048,512]{1,0:T(8,128)(2,1)} %multiply_convert_fusion.1), channel_id=1, source_target_pairs={{8,0},{16,8},{24,16},{9,1},{17,9},{25,17},{10,2},{18,10},{26,18},{... | collective-permute-start | bytes 6291464 | tf_op jit(solution)/shard_map/ppermute | solution.py:16
  20.0 213.5 %collective-permute-start.5 = (bf16[2048,512]{1,0:T(8,128)(2,1)}, bf16[2048,512]{1,0:T(8,128)(2,1)}, u32[]{:S(2)}, u32[]{:S(2)}) collective-permute-start(bf16[2048,512]{1,0:T(8,128)(2,1)} %bitcast.20), channel_id=1, source_target_pairs={{0,1},{1,2},{2,3},{3,4},{4,5},{5,6},{6,7},{8,9},{9,10},{10,11},{11... | collective-permute-start | bytes 6291464 | tf_op jit(solution)/shard_map/ppermute | solution.py:16
  31.6 203.1 %collective-permute-start.7 = (bf16[2048,512]{1,0:T(8,128)(2,1)}, bf16[2048,512]{1,0:T(8,128)(2,1)}, u32[]{:S(2)}, u32[]{:S(2)}) collective-permute-start(bf16[2048,512]{1,0:T(8,128)(2,1)} %bitcast.29), channel_id=1, source_target_pairs={{0,8},{8,16},{16,24},{1,9},{9,17},{17,25},{2,10},{10,18},{18,26},{... | collective-permute-start | bytes 6291464 | tf_op jit(solution)/shard_map/ppermute | solution.py:16
  43.9 4.2 %copy-start.15 = (f32[1,1,8192]{2,1,0:T(1,128)S(1)}, f32[1,1,8192]{2,1,0:T(1,128)}, u32[]{:S(2)}) copy-start(f32[1,1,8192]{2,1,0:T(1,128)} %param.20) | copy-start | bytes 98308
  46.5 192.7 %collective-permute-start = (bf16[2048,512]{1,0:T(8,128)(2,1)}, bf16[2048,512]{1,0:T(8,128)(2,1)}, u32[]{:S(2)}, u32[]{:S(2)}) collective-permute-start(bf16[2048,512]{1,0:T(8,128)(2,1)} %multiply_convert_fusion.2), channel_id=1, source_target_pairs={{1,0},{2,1},{3,2},{4,3},{5,4},{6,5},{7,6},{9,8},{10,9},{11,10},{12... | collective-permute-start | bytes 6291464 | tf_op jit(solution)/shard_map/ppermute | solution.py:16
  59.0 1.0 copy-start.9
  200.0 26.1 %copy-start.3 = (f32[512,256]{1,0:T(8,128)}, f32[512,256]{1,0:T(8,128)S(1)}, u32[]{:S(2)}) copy-start(f32[512,256]{1,0:T(8,128)S(1)} %bitcast_multiply_fusion) | copy-start | bytes 1572868
  202.2 13.0 %copy-start.14 = (s32[4,8,2]{1,2,0:T(2,128)S(1)}, s32[4,8,2]{1,2,0:T(2,128)}, u32[]{:S(2)}) copy-start(s32[4,8,2]{1,2,0:T(2,128)} %param.23) | copy-start | bytes 772
  203.1 23.0 %copy-start.5 = (f32[128,256]{1,0:T(8,128)}, f32[128,256]{1,0:T(8,128)S(1)}, u32[]{:S(2)}) copy-start(f32[128,256]{1,0:T(8,128)S(1)} %fusion.129) | copy-start | bytes 393220
  203.8 24.9 %copy-start.7 = (f32[128,256]{1,0:T(8,128)}, f32[128,256]{1,0:T(8,128)S(1)}, u32[]{:S(2)}) copy-start(f32[128,256]{1,0:T(8,128)S(1)} %fusion.125) | copy-start | bytes 393220
  204.6 24.1 %copy-start.10 = (f32[128,256]{1,0:T(8,128)}, f32[128,256]{1,0:T(8,128)S(1)}, u32[]{:S(2)}) copy-start(f32[128,256]{1,0:T(8,128)S(1)} %fusion.122) | copy-start | bytes 393220
  205.3 8.0 %collective-permute-start.2 = (bf16[1,1,512,256]{3,2,1,0:T(8,128)(2,1)}, bf16[1,1,512,256]{3,2,1,0:T(8,128)(2,1)}, u32[]{:S(2)}, u32[]{:S(2)}) collective-permute-start(bf16[1,1,512,256]{3,2,1,0:T(8,128)(2,1)} %convert_bitcast_fusion.1), channel_id=1, source_target_pairs={{8,0},{16,8},{24,16},{9,1},{17,9},{25,17},{10,2},{18,10},{26,18},{... | collective-permute-start | bytes 786440 | tf_op jit(solution)/shard_map/ppermute | solution.py:31
  213.3 5.5 %collective-permute-start.1 = (bf16[1,1,512,256]{3,2,1,0:T(8,128)(2,1)}, bf16[1,1,512,256]{3,2,1,0:T(8,128)(2,1)}, u32[]{:S(2)}, u32[]{:S(2)}) collective-permute-start(bf16[1,1,512,256]{3,2,1,0:T(8,128)(2,1)} %convert_bitcast_fusion.1), channel_id=1, source_target_pairs={{0,8},{8,16},{16,24},{1,9},{9,17},{17,25},{2,10},{10,18},{18,26},{... | collective-permute-start | bytes 786440 | tf_op jit(solution)/shard_map/ppermute | solution.py:30
  220.9 37.2 %collective-permute-start.6 = (bf16[3,1,512,256]{3,2,1,0:T(8,128)(2,1)}, bf16[3,1,512,256]{3,2,1,0:T(8,128)(2,1)}, u32[]{:S(2)}, u32[]{:S(2)}) collective-permute-start(bf16[3,1,512,256]{3,2,1,0:T(8,128)(2,1)} %pad_maximum_fusion), channel_id=1, source_target_pairs={{0,1},{1,2},{2,3},{3,4},{4,5},{5,6},{6,7},{8,9},{9,10},{10,11},{11... | collective-permute-start | bytes 2359304 | tf_op jit(solution)/shard_map/ppermute | solution.py:30
  228.7 31.4 %collective-permute-start.3 = (bf16[3,1,512,256]{3,2,1,0:T(8,128)(2,1)}, bf16[3,1,512,256]{3,2,1,0:T(8,128)(2,1)}, u32[]{:S(2)}, u32[]{:S(2)}) collective-permute-start(bf16[3,1,512,256]{3,2,1,0:T(8,128)(2,1)} %pad_maximum_fusion), channel_id=1, source_target_pairs={{1,0},{2,1},{3,2},{4,3},{5,4},{6,5},{7,6},{9,8},{10,9},{11,10},{12... | collective-permute-start | bytes 2359304 | tf_op jit(solution)/shard_map/ppermute | solution.py:31
  243.7 14.4 %copy-start = (f32[512,512]{1,0:T(8,128)S(1)}, f32[512,512]{1,0:T(8,128)}, u32[]{:S(2)}) copy-start(f32[512,512]{1,0:T(8,128)} %get-tuple-element.162) | copy-start | bytes 3145732
  245.3 14.8 %copy-start.2 = (f32[512,512]{1,0:T(8,128)S(1)}, f32[512,512]{1,0:T(8,128)}, u32[]{:S(2)}) copy-start(f32[512,512]{1,0:T(8,128)} %get-tuple-element.160) | copy-start | bytes 3145732
  245.3 14.8 %copy-start.12 = (f32[512,256]{1,0:T(8,128)S(1)}, f32[512,256]{1,0:T(8,128)}, u32[]{:S(2)}) copy-start(f32[512,256]{1,0:T(8,128)} %convolution_subtract_fusion.3) | copy-start | bytes 1572868
  263.3 3.1 copy-start.6
  263.3 3.1 copy-start.8
  263.3 3.1 copy-start.11
  265.5 14.3 %copy-start.4 = (f32[512,256]{1,0:T(8,128)S(1)}, f32[512,256]{1,0:T(8,128)}, u32[]{:S(2)}) copy-start(f32[512,256]{1,0:T(8,128)} %copy-done.3) | copy-start | bytes 1572868
  266.5 7.7 %collective-permute-start.9 = (bf16[1,1,512,256]{3,2,1,0:T(8,128)(2,1)S(1)}, bf16[1,1,512,256]{3,2,1,0:T(8,128)(2,1)S(1)}, u32[]{:S(2)}, u32[]{:S(2)}) collective-permute-start(bf16[1,1,512,256]{3,2,1,0:T(8,128)(2,1)S(1)} %get-tuple-element.74), channel_id=1, source_target_pairs={{8,0},{16,8},{24,16},{9,1},{17,9},{25,17},{10,2},{18,10},{26,18},{... | collective-permute-start | bytes 786440 | tf_op jit(solution)/shard_map/ppermute | solution.py:31
  270.4 5.2 %collective-permute-start.8 = (bf16[1,1,512,256]{3,2,1,0:T(8,128)(2,1)S(1)}, bf16[1,1,512,256]{3,2,1,0:T(8,128)(2,1)S(1)}, u32[]{:S(2)}, u32[]{:S(2)}) collective-permute-start(bf16[1,1,512,256]{3,2,1,0:T(8,128)(2,1)S(1)} %get-tuple-element.74), channel_id=1, source_target_pairs={{0,8},{8,16},{16,24},{1,9},{9,17},{17,25},{2,10},{10,18},{18,26},{... | collective-permute-start | bytes 786440 | tf_op jit(solution)/shard_map/ppermute | solution.py:30
  275.7 37.1 %collective-permute-start.11 = (bf16[3,1,512,256]{3,2,1,0:T(8,128)(2,1)S(1)}, bf16[3,1,512,256]{3,2,1,0:T(8,128)(2,1)S(1)}, u32[]{:S(2)}, u32[]{:S(2)}) collective-permute-start(bf16[3,1,512,256]{3,2,1,0:T(8,128)(2,1)S(1)} %pad_maximum_fusion.1), channel_id=1, source_target_pairs={{0,1},{1,2},{2,3},{3,4},{4,5},{5,6},{6,7},{8,9},{9,10},{10,11},{11... | collective-permute-start | bytes 2359304 | tf_op jit(solution)/shard_map/ppermute | solution.py:30
  279.9 3.8 %copy-start.1 = (f32[512,512]{1,0:T(8,128)S(1)}, f32[512,512]{1,0:T(8,128)}, u32[]{:S(2)}) copy-start(f32[512,512]{1,0:T(8,128)} %get-tuple-element.163) | copy-start | bytes 3145732
  281.7 32.1 %collective-permute-start.10 = (bf16[3,1,512,256]{3,2,1,0:T(8,128)(2,1)S(1)}, bf16[3,1,512,256]{3,2,1,0:T(8,128)(2,1)S(1)}, u32[]{:S(2)}, u32[]{:S(2)}) collective-permute-start(bf16[3,1,512,256]{3,2,1,0:T(8,128)(2,1)S(1)} %pad_maximum_fusion.1), channel_id=1, source_target_pairs={{1,0},{2,1},{3,2},{4,3},{5,4},{6,5},{7,6},{9,8},{10,9},{11,10},{12... | collective-permute-start | bytes 2359304 | tf_op jit(solution)/shard_map/ppermute | solution.py:31
where the time goes:
time: 326 us; the launch traced here: 320 us
  other arithmetic  139 us (43%)
  matrix products  57.1 us (18%)
  waiting for transfers between devices  47.7 us (15%)
  local copies, waits for them, and re-layouts  34.8 us (11%)
  starting transfers between devices  34.6 us (11%)
  between operations  7.28 us (2%)
    another operation x14, other arithmetic, on_device(): factor = jnp.linalg.cholesky(diagonal_block)  78.9 us
    another operation x4, other arithmetic, on_device(): coeffs = damping * jax.scipy.linalg.cho_solve((factor, True), rhs)  40.3 us
    ppermute x4, waiting for transfers between devices, extended(): before = lax.ppermute(last, axis, up)  40.3 us
    dot_general x4, matrix products, contract(): lax.dot_general(left_rows, right_rows, (((0,), (0,)), ((), ())), preferre...  22.9 us
    gather x4, local copies, waits for them, and re-layouts, interface(): return jnp.take(tiled, tile_list, axis=0).reshape(-1, tiled.shape[2])  18.9 us
    ppermute x4, starting transfers between devices, extended(): before = lax.ppermute(last, axis, up)  13.1 us
    ppermute x4, starting transfers between devices, passed_along(): return lax.ppermute(block, axis, route)  12.6 us
    another operation x13, local copies, waits for them, and re-layouts, on_device(): coeffs = damping * jax.scipy.linalg.cho_solve((factor, True), rhs)  10.7 us
  transfers between devices with their start and end apart: 12, of which 6 were waited for; matrix products, arithmetic and copies ran while one was open for 64% of the time, Pallas kernels for 0%

commit v1 on v0

v1 whole, which is shorter than its diff:
```python
import functools

import jax
import jax.numpy as jnp
from jax import lax
from jax.experimental import pallas as pl
from jax.experimental.pallas import tpu as pltpu
from jax.sharding import PartitionSpec as P

TILE = 128
ITERS = 3
HALO = 16
damping = 0.8
MESH = pl.DeviceIdType.MESH
F32 = jnp.float32
BF16 = jnp.bfloat16
VMEM = pl.BlockSpec(memory_space=pltpu.VMEM)
SMEM = pl.BlockSpec(memory_space=pltpu.SMEM)
ANY = pl.BlockSpec(memory_space=pl.ANY)


def dot(a, b):
    return jnp.dot(a, b, preferred_element_type=F32)


def dot_t(a, b):
    return lax.dot_general(a, b, (((0,), (0,)), ((), ())), preferred_element_type=F32)


def split(a):
    high = a.astype(BF16)
    return high, (a - high.astype(F32)).astype(BF16)


def dot3(a, b):
    return dot(a[0], b[0]) + (dot(a[0], b[1]) + dot(a[1], b[0]))


def tile_copy(ids_ref, side, basis_ref, rows_ref, offset, sems, t):
    return pltpu.make_async_copy(
        basis_ref.at[pl.ds(pl.multiple_of(ids_ref[side, t] * TILE, TILE), TILE), :],
        rows_ref.at[pl.ds(offset + t * TILE, TILE), :],
        sems.at[t],
    )


def image_kernel(side, ids_ref, basis_ref, weight_ref, out_ref, rows_ref, sems):
    tiles = out_ref.shape[0] // TILE
    width = out_ref.shape[1]
    for t in range(tiles):
        tile_copy(ids_ref, side, basis_ref, rows_ref, HALO, sems, t).start()
    zero = jnp.zeros((HALO, width), BF16)
    rows_ref[pl.ds(0, HALO), :] = zero
    rows_ref[pl.ds(HALO + tiles * TILE, HALO), :] = zero
    for t in range(tiles):
        tile_copy(ids_ref, side, basis_ref, rows_ref, HALO, sems, t).wait()

    @pl.loop(0, tiles)
    def _(t):
        start = pl.multiple_of(t * TILE, TILE)
        values = rows_ref[pl.ds(start, TILE + 2 * HALO), :].astype(F32)
        scale = jnp.broadcast_to(weight_ref[pl.ds(t, 1), :], (TILE, TILE)).T
        scale = jnp.concatenate([scale] * (width // TILE), axis=1)
        here = values[HALO : HALO + TILE]
        before = values[HALO - 1 : HALO - 1 + TILE]
        after = values[HALO + 1 : HALO + 1 + TILE]
        out_ref[pl.ds(start, TILE), :] = (scale * (2.5 * here - before - after)).astype(BF16)


def image_of(side, tile_ids, basis, weight):
    rows, width = weight.shape[0], basis.shape[1]
    tiles = rows // TILE
    return pl.pallas_call(
        functools.partial(image_kernel, side),
        out_shape=jax.ShapeDtypeStruct((rows, width), BF16),
        in_specs=[SMEM, ANY, VMEM],
        out_specs=VMEM,
        scratch_shapes=[
            pltpu.VMEM((rows + 2 * HALO, width), BF16),
            pltpu.SemaphoreType.DMA((tiles,)),
        ],
        cost_estimate=pl.CostEstimate(
            flops=8 * rows * width, bytes_accessed=4 * rows * width, transcendentals=0
        ),
        name="image",
    )(tile_ids, basis, weight.reshape(tiles, TILE))


def block_kernel(side, ids_ref, live_ref, basis_ref, image_ref, out_ref, rows_ref, sems):
    tiles = rows_ref.shape[0] // TILE
    for t in range(tiles):
        tile_copy(ids_ref, side, basis_ref, rows_ref, 0, sems, t).start()
    for t in range(tiles):
        tile_copy(ids_ref, side, basis_ref, rows_ref, 0, sems, t).wait()
    block = dot_t(rows_ref[...], image_ref[...])
    live = jnp.full(block.shape, live_ref[0], jnp.int32) > 0
    out_ref[...] = jnp.where(live, block, 0.0).astype(BF16)


def block_of(side, tile_ids, live, basis, image):
    rows, width = image.shape
    tiles = rows // TILE
    return pl.pallas_call(
        functools.partial(block_kernel, side),
        out_shape=jax.ShapeDtypeStruct((width, width), BF16),
        in_specs=[SMEM, SMEM, ANY, VMEM],
        out_specs=VMEM,
        scratch_shapes=[
            pltpu.VMEM((rows, width), BF16),
            pltpu.SemaphoreType.DMA((tiles,)),
        ],
        cost_estimate=pl.CostEstimate(
            flops=2 * rows * width * width, bytes_accessed=4 * rows * width, transcendentals=0
        ),
        name="block",
    )(tile_ids, live.astype(jnp.int32).reshape(1), basis, image)


def diagonal_kernel(count_ref, basis_ref, weight_ref, loads_ref, inv_ref, first_ref, a_ref, x_ref):
    step = pl.program_id(0)
    width = a_ref.shape[0]
    half = width // 2

    @pl.when(step == 0)
    def _():
        a_ref[...] = jnp.zeros_like(a_ref)

    rows = basis_ref[...]
    turned = rows.T
    pieces = []
    for t in range(weight_ref.shape[0]):
        piece = turned[:, t * TILE : (t + 1) * TILE].astype(F32)
        pieces.append((piece * weight_ref[pl.ds(t, 1), :]).astype(BF16))
    weighted = jnp.concatenate(pieces, axis=1)
    a_ref[:half, :] += dot(weighted[:half], rows)
    a_ref[half:, half:] += dot(weighted[half:], rows[:, half:])

    @pl.when(step == pl.num_programs(0) - 1)
    def _():
        a_ref[half:, :half] = a_ref[:half, half:].T
        a = a_ref[...]
        row_at = lax.broadcasted_iota(jnp.int32, a.shape, 0)
        col_at = lax.broadcasted_iota(jnp.int32, a.shape, 1)
        eye = jnp.where(row_at == col_at, 1.0, 0.0).astype(F32)
        bound = jnp.max(jnp.sum(jnp.abs(a), axis=0, keepdims=True))
        split_a = split(a)
        low = 0.004
        scale = 2.0 / (1.0 + low)
        alpha = scale / bound
        low = scale * low
        low = 1.0 - (1.0 - low) ** 2
        scale = 2.0 / (1.0 + low)
        low = scale * low
        x_ref[...] = scale * alpha * (2.0 * eye - alpha * a)

        def coarse(i, low):
            low = low * (2.0 - low)
            scale = 2.0 / (1.0 + low)
            x = x_ref[...]
            xb = x.astype(BF16)
            t = dot(split_a[0], xb)
            x_ref[...] = scale * (2.0 * x - dot(xb, t.astype(BF16)))
            return low * scale

        lax.fori_loop(0, 5, coarse, jnp.float32(low))

        def fine(state):
            i, _ = state
            x = x_ref[...]
            split_x = split(x)
            r = eye - dot3(split_a, split_x)
            size = jnp.sum(r * r)
            moved = x + dot3(split_x, split(r))
            restart = jnp.logical_and(i == 0, jnp.logical_not(size < 1.0))
            take = jnp.full(x.shape, restart.astype(jnp.int32), jnp.int32) > 0
            x_ref[...] = jnp.where(take, eye / bound, moved)
            return i + 1, size

        lax.while_loop(
            lambda s: jnp.logical_and(
                s[0] < 48, jnp.logical_or(s[0] < 2 - (s[1] < 1.0).astype(jnp.int32), s[1] >= 0.01)
            ),
            fine,
            (jnp.int32(0), jnp.float32(1.0)),
        )
        inverse = x_ref[...].astype(BF16)
        inv_ref[...] = inverse
        loads = loads_ref[...]
        column = lax.broadcasted_iota(jnp.int32, loads.shape, 1)
        rhs = jnp.where(column < count_ref[0], loads, 0.0)
        y = dot(inverse, rhs.astype(BF16))
        y = y + dot(inverse, (rhs - dot3(split_a, split(y))).astype(BF16))
        first_ref[...] = damping * y


def diagonal_of(count, basis, weight, loads):
    rows, width = basis.shape
    columns = loads.shape[1]
    chunk = 1024
    return pl.pallas_call(
        diagonal_kernel,
        grid=(rows // chunk,),
        out_shape=(
            jax.ShapeDtypeStruct((width, width), BF16),
            jax.ShapeDtypeStruct((width, columns), F32),
        ),
        in_specs=[
            SMEM,
            pl.BlockSpec((chunk, width), lambda i: (i, 0)),
            pl.BlockSpec((chunk // TILE, TILE), lambda i: (i, 0)),
            pl.BlockSpec((width, columns), lambda i: (0, 0)),
        ],
        out_specs=(
            pl.BlockSpec((width, width), lambda i: (0, 0)),
            pl.BlockSpec((width, columns), lambda i: (0, 0)),
        ),
        scratch_shapes=[pltpu.VMEM((width, width), F32), pltpu.VMEM((width, width), F32)],
        compiler_params=pltpu.CompilerParams(dimension_semantics=("arbitrary",)),
        cost_estimate=pl.CostEstimate(
            flops=2 * rows * width * width + 40 * width**3,
            bytes_accessed=2 * rows * width,
            transcendentals=0,
        ),
        name="diagonal",
    )(count, basis, weight.reshape(rows // TILE, TILE), loads)


def sweep_kernel(
    n_sx, n_sy, inv_ref, first_ref, east_ref, south_ref, out_ref, own, for_east, for_south,
    got, total, send_sem, recv_sem,
):
    row, col = lax.axis_index("sx"), lax.axis_index("sy")
    west = (col > 0, (row, col - 1))
    north = (row > 0, (row - 1, col))
    east = (col < n_sy - 1, (row, col + 1))
    south = (row < n_sx - 1, (row + 1, col))
    sides = (west, north, east, south)
    barrier = pltpu.get_barrier_semaphore()
    present = jnp.int32(0)
    for there, place in sides:
        present = present + there.astype(jnp.int32)

        @pl.when(there)
        def _():
            pl.semaphore_signal(barrier, inc=1, device_id=place, device_id_type=MESH)

    pl.semaphore_wait(barrier, present)

    def copy_to(sweep, side):
        source = (own, own, for_east, for_south)[side]
        return pltpu.make_async_remote_copy(
            src_ref=source.at[sweep],
            dst_ref=got.at[sweep, (side + 2) % 4],
            send_sem=send_sem.at[sweep, side],
            recv_sem=recv_sem.at[sweep, (side + 2) % 4],
            device_id=sides[side][1],
            device_id_type=MESH,
        )

    def arrival(sweep, side):
        return pltpu.make_async_remote_copy(
            src_ref=got.at[sweep, side],
            dst_ref=got.at[sweep, side],
            send_sem=send_sem.at[sweep, side],
            recv_sem=recv_sem.at[sweep, side],
            device_id=sides[side][1],
            device_id_type=MESH,
        )

    def send(sweep, side):
        @pl.when(sides[side][0])
        def _():
            copy_to(sweep, side).start()

    out_ref[...] = first_ref[...]
    for sweep in range(ITERS - 1):
        coeffs = out_ref[...].astype(BF16)
        own[sweep] = coeffs
        for_east[sweep] = dot_t(east_ref[...], coeffs).astype(BF16)
        send(sweep, 0)
        send(sweep, 1)
        for_south[sweep] = dot_t(south_ref[...], coeffs).astype(BF16)
        send(sweep, 2)
        send(sweep, 3)
        total[...] = jnp.zeros_like(total)
        for side in (1, 3, 0, 2):
            @pl.when(sides[side][0])
            def _():
                arrival(sweep, side).wait_recv()
                value = got[sweep, side]
                if side == 2:
                    total[...] += dot(east_ref[...], value)
                elif side == 3:
                    total[...] += dot(south_ref[...], value)
                else:
                    total[...] += value.astype(F32)

        out_ref[...] = (
            (1.0 - damping) * out_ref[...]
            + first_ref[...]
            - damping * dot(inv_ref[...], total[...].astype(BF16))
        )
    for sweep in range(ITERS - 1):
        for side in range(4):
            @pl.when(sides[side][0])
            def _():
                copy_to(sweep, side).wait_send()


def sweeps_of(n_sx, n_sy, inverse, first, east, south):
    shape = first.shape
    further = ITERS - 1
    return pl.pallas_call(
        functools.partial(sweep_kernel, n_sx, n_sy),
        out_shape=jax.ShapeDtypeStruct(shape, F32),
        in_specs=[VMEM] * 4,
        out_specs=VMEM,
        scratch_shapes=[
            pltpu.VMEM((further,) + shape, BF16),
            pltpu.VMEM((further,) + shape, BF16),
            pltpu.VMEM((further,) + shape, BF16),
            pltpu.VMEM((further, 4) + shape, BF16),
            pltpu.VMEM(shape, F32),
            pltpu.SemaphoreType.DMA((further, 4)),
            pltpu.SemaphoreType.DMA((further, 4)),
        ],
        compiler_params=pltpu.CompilerParams(collective_id=0, has_side_effects=True),
        name="sweeps",
    )(inverse, first, east, south)


def moved_back(block, axis, peers):
    return lax.ppermute(block, axis, [(i + 1, i) for i in range(peers - 1)])


def solution(mesh):
    n_sx, n_sy = mesh.shape["sx"], mesh.shape["sy"]

    def on_device(basis, diag_weight, correlation_weight, tile_ids, pair_live, loads, load_count):
        basis = basis[0, 0]
        ids = tile_ids[0, 0]
        row_at, col_at = lax.axis_index("sx"), lax.axis_index("sy")
        live = pair_live[row_at, col_at]
        live_east = jnp.logical_and(live[0] > 0, col_at < n_sy - 1)
        live_south = jnp.logical_and(live[1] > 0, row_at < n_sx - 1)
        image_west = image_of(0, ids, basis, correlation_weight[0, 0, 0])
        from_east = moved_back(image_west, "sy", n_sy)
        image_north = image_of(2, ids, basis, correlation_weight[0, 0, 1])
        from_south = moved_back(image_north, "sx", n_sx)
        inverse, first = diagonal_of(load_count[0], basis, diag_weight[0, 0], loads[0, 0])
        block_south = block_of(3, ids, live_south, basis, from_south)
        block_east = block_of(1, ids, live_east, basis, from_east)
        coeffs = sweeps_of(n_sx, n_sy, inverse, first, block_east, block_south)
        return coeffs[None, None]

    return jax.shard_map(
        on_device,
        mesh=mesh,
        in_specs=(
            P("sx", "sy", None, None),
            P("sx", "sy", None),
            P("sx", "sy", None, None),
            P("sx", "sy", None, None),
            P(),
            P("sx", "sy", None, None),
            P("sx", "sy"),
        ),
        out_specs=P("sx", "sy", None, None),
        check_vma=False,
    )
```

time: 326 us -> 106 us (0.33)
  the two profiles are of different devices: /device:TPU:1 before, /device:TPU:10 now
where the time goes in v1:
time: 106 us; the launch traced here: 105 us
  Pallas kernels  73.6 us (69%)
  waiting for transfers between devices  20.3 us (19%)
  local copies, waits for them, and re-layouts  5.2 us (5%)
  starting transfers between devices  3.74 us (4%)
  between operations  2.03 us (2%)
    pallas_call x1, Pallas kernels, sweeps_of(): pl.pallas_call(functools.partial(sweep_kernel, n_sx, n_sy), out_shape=jax...  32.3 us
    ppermute x2, waiting for transfers between devices, moved_back(): return lax.ppermute(block, axis, [(i + 1, i) for i in range(peers - 1)])  20.3 us
    pallas_call x1, Pallas kernels, diagonal_of(): pl.pallas_call(diagonal_kernel, grid=(rows // chunk,), out_shape=(jax.Sha...  19.4 us
    pallas_call x2, Pallas kernels, image_of(): pl.pallas_call(functools.partial(image_kernel, side), out_shape=jax.Shape...  11.1 us
    pallas_call x2, Pallas kernels, block_of(): pl.pallas_call(functools.partial(block_kernel, side), out_shape=jax.Shape...  10.8 us
    ppermute x2, starting transfers between devices, moved_back(): return lax.ppermute(block, axis, [(i + 1, i) for i in range(peers - 1)])  3.74 us
    unnamed x5, local copies, waits for them, and re-layouts  3.18 us
  transfers between devices with their start and end apart: 2, of which 1 were waited for; matrix products, arithmetic and copies ran while one was open for 1% of the time, Pallas kernels for 29%

profile of v1, /device:TPU:10, one launch (start us, length us, event | category | flops | bytes accessed | tf_op | source)
XLA Modules:
  0.0 104.9 jit_solution(4590683757439531531)
XLA Ops:
  0.0 0.0 copy-start
  0.0 1.4 %fusion = (f32[1,1,1,2048]{3,2,1,0:T(1,128)}, f32[1,1,1,2048]{3,2,1,0:T(1,128)}) fusion(f32[1,1,2,2048]{3,2,1,0:T(2,128)} %param.9), kind=kLoop, calls=%fused_computation.1 | loop fusion | bytes 32768 | tf_op jit(solution)/shard_map/slice | solution.py:348
  1.4 5.5 %image.3 = bf16[2048,512]{1,0:T(8,128)(2,1)} custom-call(s32[4,16]{1,0:T(4,128)} %bitcast.19, bf16[8192,512]{1,0:T(8,128)(2,1)} %bitcast.13, f32[16,128]{1,0:T(8,128)} %bitcast.24), custom_call_target="tpu_custom_call" | custom-call | flops 8388608 | bytes 4194304 | tf_op jit(solution)/shard_map/image/pallas_call | solution.py:73
  6.9 1.3 %collective-permute-start.1 = (bf16[2048,512]{1,0:T(8,128)(2,1)}, bf16[2048,512]{1,0:T(8,128)(2,1)S(1)}, u32[]{:S(2)}, u32[]{:S(2)}) collective-permute-start(bf16[2048,512]{1,0:T(8,128)(2,1)} %image.3), channel_id=1, source_target_pairs={{8,0},{16,8},{24,16},{9,1},{17,9},{25,17},{10,2},{18,10},{26,18},{... | collective-permute-start | bytes 6291464 | tf_op jit(solution)/shard_map/ppermute | solution.py:333
  8.2 5.6 %image.2 = bf16[2048,512]{1,0:T(8,128)(2,1)} custom-call(s32[4,16]{1,0:T(4,128)} %bitcast.20, bf16[8192,512]{1,0:T(8,128)(2,1)} %bitcast.14, f32[16,128]{1,0:T(8,128)} %bitcast.23), custom_call_target="tpu_custom_call" | custom-call | flops 8388608 | bytes 4194304 | tf_op jit(solution)/shard_map/image/pallas_call | solution.py:73
  13.8 2.4 %collective-permute-start = (bf16[2048,512]{1,0:T(8,128)(2,1)}, bf16[2048,512]{1,0:T(8,128)(2,1)}, u32[]{:S(2)}, u32[]{:S(2)}) collective-permute-start(bf16[2048,512]{1,0:T(8,128)(2,1)} %image.2), channel_id=1, source_target_pairs={{1,0},{2,1},{3,2},{4,3},{5,4},{6,5},{7,6},{9,8},{10,9},{11,10},{12... | collective-permute-start | bytes 6291464 | tf_op jit(solution)/shard_map/ppermute | solution.py:333
  16.3 0.0 copy-done
  16.3 0.1 constant_dynamic-slice_fusion
  16.4 0.5 fusion.1
  18.8 19.4 %diagonal.1 = (bf16[512,512]{1,0:T(8,128)(2,1)}, f32[512,256]{1,0:T(8,128)}) custom-call(s32[1]{0:T(128)} %bitcast.12.count_ref, bf16[8192,512]{1,0:T(8,128)(2,1)} %bitcast.15, f32[64,128]{1,0:T(8,128)} %bitcast.26, f32[512,256]{1,0:T(8,128)} %bitcast.25), custom_call_target="tpu_custom_call" | custom-call | flops 9663676416 | bytes 8388608 | tf_op jit(solution)/shard_map/diagonal/pallas_call | solution.py:200
  38.2 0.0 collective-permute-done.1.image_ref
  38.2 0.0 copy-start.1
  38.2 1.3 %copy-done.1 = bf16[2048,512]{1,0:T(8,128)(2,1)} copy-done((bf16[2048,512]{1,0:T(8,128)(2,1)}, bf16[2048,512]{1,0:T(8,128)(2,1)S(1)}, u32[]{:S(2)}) %copy-start.1) | copy-done | bytes 2097176
  39.5 5.4 %block.3.south_ref = bf16[512,512]{1,0:T(8,128)(2,1)} custom-call(s32[4,16]{1,0:T(4,128)} %bitcast.21, s32[1]{0:T(128)} %bitcast.9.live_ref, bf16[8192,512]{1,0:T(8,128)(2,1)} %bitcast.16, bf16[2048,512]{1,0:T(8,128)(2,1)} %copy-done.1), custom_call_target="tpu_custom_call" | custom-call | flops 1073741824 | bytes 4194304 | tf_op jit(solution)/shard_map/block/pallas_call | solution.py:103
  45.0 20.3 %collective-permute-done.image_ref = bf16[2048,512]{1,0:T(8,128)(2,1)} collective-permute-done((bf16[2048,512]{1,0:T(8,128)(2,1)}, bf16[2048,512]{1,0:T(8,128)(2,1)}, u32[]{:S(2)}, u32[]{:S(2)}) %collective-permute-start) | collective-permute-done | bytes 2097184 | tf_op jit(solution)/shard_map/ppermute | solution.py:333
  65.3 5.4 %block.2.east_ref = bf16[512,512]{1,0:T(8,128)(2,1)} custom-call(s32[4,16]{1,0:T(4,128)} %bitcast.22, s32[1]{0:T(128)} %bitcast.6.live_ref, bf16[8192,512]{1,0:T(8,128)(2,1)} %bitcast.17, bf16[2048,512]{1,0:T(8,128)(2,1)} %collective-permute-done.image_ref), custom_call_target="tpu_custom_call" | custom-call | flops 1073741824 | bytes 4194304 | tf_op jit(solution)/shard_map/block/pallas_call | solution.py:103
  70.7 32.3 %sweeps.1 = f32[512,256]{1,0:T(8,128)} custom-call(bf16[512,512]{1,0:T(8,128)(2,1)} %get-tuple-element.7.inv_ref, f32[512,256]{1,0:T(8,128)} %get-tuple-element.8.first_ref, bf16[512,512]{1,0:T(8,128)(2,1)} %block.2.east_ref, bf16[512,512]{1,0:T(8,128)(2,1)} %block.3.south_ref), custom_call_target="tpu_custom_call" | custom-call | tf_op jit(solution)/shard_map/sweeps/pallas_call | solution.py:313
  103.0 1.9 %copy.10 = f32[1,1,512,256]{3,2,1,0:T(8,128)} copy(f32[1,1,512,256]{3,2,1,0:T(8,128)} %bitcast.18) | data formatting | bytes 1048576
Async XLA Ops:
  0.0 16.3 %copy-start = (s32[4,8,2]{1,2,0:T(2,128)S(1)}, s32[4,8,2]{1,2,0:T(2,128)}, u32[]{:S(2)}) copy-start(s32[4,8,2]{1,2,0:T(2,128)} %param.11) | copy-start | bytes 772
  6.9 31.3 %collective-permute-start.1 = (bf16[2048,512]{1,0:T(8,128)(2,1)}, bf16[2048,512]{1,0:T(8,128)(2,1)S(1)}, u32[]{:S(2)}, u32[]{:S(2)}) collective-permute-start(bf16[2048,512]{1,0:T(8,128)(2,1)} %image.3), channel_id=1, source_target_pairs={{8,0},{16,8},{24,16},{9,1},{17,9},{25,17},{10,2},{18,10},{26,18},{... | collective-permute-start | bytes 6291464 | tf_op jit(solution)/shard_map/ppermute | solution.py:333
  13.8 51.5 %collective-permute-start = (bf16[2048,512]{1,0:T(8,128)(2,1)}, bf16[2048,512]{1,0:T(8,128)(2,1)}, u32[]{:S(2)}, u32[]{:S(2)}) collective-permute-start(bf16[2048,512]{1,0:T(8,128)(2,1)} %image.2), channel_id=1, source_target_pairs={{1,0},{2,1},{3,2},{4,3},{5,4},{6,5},{7,6},{9,8},{10,9},{11,10},{12... | collective-permute-start | bytes 6291464 | tf_op jit(solution)/shard_map/ppermute | solution.py:333
  38.2 1.3 %copy-start.1 = (bf16[2048,512]{1,0:T(8,128)(2,1)}, bf16[2048,512]{1,0:T(8,128)(2,1)S(1)}, u32[]{:S(2)}) copy-start(bf16[2048,512]{1,0:T(8,128)(2,1)S(1)} %collective-permute-done.1.image_ref) | copy-start | bytes 6291460

commit v2 on v1

v2 whole, which is shorter than its diff:
```python
import functools

import jax
import jax.numpy as jnp
from jax import lax
from jax.experimental import pallas as pl
from jax.experimental.pallas import tpu as pltpu
from jax.sharding import PartitionSpec as P

TILE = 128
ITERS = 3
HALO = 16
damping = 0.8
MESH = pl.DeviceIdType.MESH
F32 = jnp.float32
BF16 = jnp.bfloat16
VMEM = pl.BlockSpec(memory_space=pltpu.VMEM)
SMEM = pl.BlockSpec(memory_space=pltpu.SMEM)
ANY = pl.BlockSpec(memory_space=pl.ANY)


def dot(a, b):
    return jnp.dot(a, b, preferred_element_type=F32)


def dot_t(a, b):
    return lax.dot_general(a, b, (((0,), (0,)), ((), ())), preferred_element_type=F32)


def split(a):
    high = a.astype(BF16)
    return high, (a - high.astype(F32)).astype(BF16)


def dot3(a, b):
    return dot(a[0], b[0]) + (dot(a[0], b[1]) + dot(a[1], b[0]))


def tile_of(basis_ref, ids_ref, side, t):
    return basis_ref[ids_ref[side, t]]


def image_tile(basis_ref, ids_ref, side, t, tiles, scale):
    width = basis_ref.shape[2]
    scale = jnp.broadcast_to(scale, (TILE, TILE)).T
    scale = jnp.concatenate([scale] * (width // TILE), axis=1)
    before = ids_ref[side, lax.rem(t + tiles - 1, tiles)]
    after = ids_ref[side, lax.rem(t + 1, tiles)]
    first = basis_ref[before, TILE - HALO :, :].astype(F32)
    last = basis_ref[after, :HALO, :].astype(F32)
    first = first * (t > 0).astype(F32)
    last = last * (t < tiles - 1).astype(F32)
    here = tile_of(basis_ref, ids_ref, side, t).astype(F32)
    values = jnp.concatenate([first, here, last], axis=0)
    before = values[HALO - 1 : HALO - 1 + TILE]
    after = values[HALO + 1 : HALO + 1 + TILE]
    return (scale * (2.5 * here - before - after)).astype(BF16)


def eye_like(a):
    row_at = lax.broadcasted_iota(jnp.int32, a.shape, 0)
    col_at = lax.broadcasted_iota(jnp.int32, a.shape, 1)
    return jnp.where(row_at == col_at, 1.0, 0.0).astype(F32)


def norm_bound(a):
    return jnp.max(jnp.sum(jnp.abs(a), axis=0, keepdims=True), axis=1, keepdims=True)


def fine_step(split_a, x):
    split_x = split(x)
    r = eye_like(x) - dot3(split_a, split_x)
    return x + dot3(split_x, split(r)), jnp.sum(r * r, axis=0, keepdims=True)


def first_coeffs(split_a, inverse, loads, carried):
    rhs = loads * carried
    y = dot(inverse, rhs.astype(BF16))
    y = y + dot(inverse, (rhs - dot3(split_a, split(y))).astype(BF16))
    return damping * y


def neighbours(n_sx, n_sy):
    row, col = lax.axis_index("sx"), lax.axis_index("sy")
    west = (col > 0, (row, col - 1))
    north = (row > 0, (row - 1, col))
    east = (col < n_sy - 1, (row, col + 1))
    south = (row < n_sx - 1, (row + 1, col))
    return west, north, east, south


def meet(sides):
    barrier = pltpu.get_barrier_semaphore()
    present = jnp.int32(0)
    for there, place in sides:
        present = present + there.astype(jnp.int32)

        @pl.when(there)
        def _():
            pl.semaphore_signal(barrier, inc=1, device_id=place, device_id_type=MESH)

    pl.semaphore_wait(barrier, present)


def assemble_kernel(
    n_sx, n_sy, ids_ref, live_ref, count_ref, basis_ref, corr_ref, weight_ref, loads_ref,
    a_out, x_out, size_ref, inv_ref, first_ref, east_ref, south_ref,
    a_ref, x_ref, block_ref, sent, got, send_sem, recv_sem, local_sem,
):
    rows, width = basis_ref.shape[0] * TILE, basis_ref.shape[2]
    half = width // 2
    tiles = corr_ref.shape[1]
    per = 2 if tiles % 2 == 0 else 1
    chunk = per * TILE
    chunks = tiles // per
    sides = neighbours(n_sx, n_sy)
    meet(sides)

    def piece(which, q, peer):
        at = pl.ds(pl.multiple_of(q * chunk, chunk), chunk)
        return pltpu.make_async_remote_copy(
            src_ref=sent.at[which, at, :],
            dst_ref=got.at[which, at, :],
            send_sem=send_sem.at[which, q],
            recv_sem=recv_sem.at[which, q],
            device_id=sides[peer][1],
            device_id_type=MESH,
        )

    for which in range(2):

        @pl.when(sides[which][0])
        def _():
            @pl.loop(0, chunks)
            def _(q):
                for k in range(per):
                    t = q * per + k
                    at = pl.ds(pl.multiple_of(t * TILE, TILE), TILE)
                    sent[which, at, :] = image_tile(
                        basis_ref, ids_ref, 2 * which, t, tiles, corr_ref[which, pl.ds(t, 1), :]
                    )
                piece(which, q, which).start()

    a_ref[...] = jnp.zeros_like(a_ref)
    step_tiles = 8
    step_rows = step_tiles * TILE

    @pl.loop(0, rows // step_rows)
    def _(i):
        part = basis_ref[pl.ds(i * step_tiles, step_tiles)].reshape(step_rows, width)
        scale = weight_ref[pl.ds(pl.multiple_of(i * step_tiles, step_tiles), step_tiles), :]
        turned = part.T
        pieces = []
        for t in range(step_tiles):
            tile = turned[:, t * TILE : (t + 1) * TILE].astype(F32)
            pieces.append((tile * scale[t : t + 1, :]).astype(BF16))
        weighted = jnp.concatenate(pieces, axis=1)
        a_ref[:half, :] += dot(weighted[:half], part)
        a_ref[half:, half:] += dot(weighted[half:], part[:, half:])

    a_ref[half:, :half] = a_ref[:half, half:].T
    a_copy = pltpu.make_async_copy(a_ref, a_out, local_sem.at[0])
    a_copy.start()
    a = a_ref[...]
    bound = norm_bound(a)
    split_a = split(a)
    low = 0.004
    scale = 2.0 / (1.0 + low)
    alpha = scale / bound
    low = scale * low
    low = low * (2.0 - low)
    scale = 2.0 / (1.0 + low)
    low = scale * low
    x_ref[...] = (scale * alpha) * (2.0 * eye_like(a) - alpha * a)

    def coarse(i, low):
        low = low * (2.0 - low)
        scale = 2.0 / (1.0 + low)
        x = x_ref[...]
        xb = x.astype(BF16)
        t = dot(split_a[0], xb)
        x_ref[...] = scale * (2.0 * x - dot(xb, t.astype(BF16)))
        return low * scale

    lax.fori_loop(0, 5, coarse, jnp.float32(low))

    @pl.loop(0, 2)
    def _(i):
        x, size = fine_step(split_a, x_ref[...])
        x_ref[...] = x
        size_ref[...] = size

    x_copy = pltpu.make_async_copy(x_ref, x_out, local_sem.at[1])
    x_copy.start()
    inverse = x_ref[...].astype(BF16)
    inv_ref[...] = inverse
    first_ref[...] = first_coeffs(split_a, inverse, loads_ref[...], count_ref[...])

    for which, out_ref in ((1, south_ref), (0, east_ref)):
        block_ref[...] = jnp.zeros_like(block_ref)

        @pl.when(sides[which + 2][0])
        def _():
            @pl.loop(0, chunks)
            def _(q):
                piece(which, q, which + 2).wait_recv()
                at = pl.ds(pl.multiple_of(q * chunk, chunk), chunk)
                mine = jnp.concatenate(
                    [
                        tile_of(basis_ref, ids_ref, 2 * which + 1, q * per + k)
                        for k in range(per)
                    ],
                    axis=0,
                )
                block_ref[...] += dot_t(mine, got[which, at, :])

        out_ref[...] = (block_ref[...] * live_ref[which]).astype(BF16)

    for which in range(2):

        @pl.when(sides[which][0])
        def _():
            @pl.loop(0, chunks)
            def _(q):
                piece(which, q, which).wait_send()

    a_copy.wait()
    x_copy.wait()


def assemble(n_sx, n_sy, ids, live, count, basis, corr, weight, loads):
    rows, width = basis.shape
    overlap = corr.shape[1]
    tiles = overlap // TILE
    chunks = tiles // 2 if tiles % 2 == 0 else tiles
    square = jax.ShapeDtypeStruct((width, width), F32)
    short = jax.ShapeDtypeStruct((width, width), BF16)
    return pl.pallas_call(
        functools.partial(assemble_kernel, n_sx, n_sy),
        out_shape=(
            square, square, jax.ShapeDtypeStruct((1, width), F32), short,
            jax.ShapeDtypeStruct(loads.shape, F32), short, short,
        ),
        in_specs=[SMEM, SMEM, VMEM, VMEM, VMEM, VMEM, VMEM],
        out_specs=(ANY, ANY, VMEM, VMEM, VMEM, VMEM, VMEM),
        scratch_shapes=[
            pltpu.VMEM((width, width), F32),
            pltpu.VMEM((width, width), F32),
            pltpu.VMEM((width, width), F32),
            pltpu.VMEM((2, overlap, width), BF16),
            pltpu.VMEM((2, overlap, width), BF16),
            pltpu.SemaphoreType.DMA((2, chunks)),
            pltpu.SemaphoreType.DMA((2, chunks)),
            pltpu.SemaphoreType.DMA((2,)),
        ],
        compiler_params=pltpu.CompilerParams(collective_id=1, has_side_effects=True),
        name="assemble",
    )(
        ids, live, count, basis.reshape(rows // TILE, TILE, width), corr.reshape(2, tiles, TILE),
        weight.reshape(rows // TILE, TILE), loads,
    )


def finish_kernel(
    count_ref, size_ref, a_hbm, x_hbm, loads_hbm, inv_in, first_in, inv_out, first_out,
    a_ref, x_ref, loads_ref, inv_ref, first_ref, sems,
):
    size = jnp.sum(size_ref[...])

    @pl.when(jnp.logical_not(size < 0.01))
    def _():
        inputs = [
            pltpu.make_async_copy(source, target, sems.at[k])
            for k, (source, target) in enumerate(
                ((a_hbm, a_ref), (x_hbm, x_ref), (loads_hbm, loads_ref))
            )
        ]
        for copy in inputs:
            copy.start()
        for copy in inputs:
            copy.wait()
        a = a_ref[...]
        split_a = split(a)

        @pl.when(jnp.logical_not(size < 1.0))
        def _():
            x_ref[...] = eye_like(a) / norm_bound(a)

        def step(state):
            i, _ = state
            x, size = fine_step(split_a, x_ref[...])
            x_ref[...] = x
            return i + 1, jnp.sum(size)

        lax.while_loop(
            lambda s: jnp.logical_and(s[0] < 48, s[1] >= 0.0001),
            step,
            (jnp.int32(0), jnp.float32(1.0)),
        )
        inverse = x_ref[...].astype(BF16)
        inv_ref[...] = inverse
        first_ref[...] = first_coeffs(split_a, inverse, loads_ref[...], count_ref[...])
        outputs = [
            pltpu.make_async_copy(inv_ref, inv_out, sems.at[3]),
            pltpu.make_async_copy(first_ref, first_out, sems.at[4]),
        ]
        for copy in outputs:
            copy.start()
        for copy in outputs:
            copy.wait()


def finish(count, size, a, x, loads, inverse, first):
    square = pltpu.VMEM(a.shape, F32)
    return pl.pallas_call(
        finish_kernel,
        out_shape=(
            jax.ShapeDtypeStruct(inverse.shape, BF16), jax.ShapeDtypeStruct(first.shape, F32),
        ),
        in_specs=[VMEM, VMEM, ANY, ANY, ANY, ANY, ANY],
        out_specs=(ANY, ANY),
        scratch_shapes=[
            square, square, pltpu.VMEM(loads.shape, F32), pltpu.VMEM(inverse.shape, BF16),
            pltpu.VMEM(first.shape, F32), pltpu.SemaphoreType.DMA((5,)),
        ],
        input_output_aliases={5: 0, 6: 1},
        name="finish",
    )(count, size, a, x, loads, inverse, first)


def sweep_kernel(
    n_sx, n_sy, inv_ref, first_ref, east_ref, south_ref, out_ref, own, for_east, for_south,
    got, total, send_sem, recv_sem,
):
    sides = neighbours(n_sx, n_sy)
    meet(sides)

    def copy_to(sweep, side):
        source = (own, own, for_east, for_south)[side]
        return pltpu.make_async_remote_copy(
            src_ref=source.at[sweep],
            dst_ref=got.at[sweep, (side + 2) % 4],
            send_sem=send_sem.at[sweep, side],
            recv_sem=recv_sem.at[sweep, (side + 2) % 4],
            device_id=sides[side][1],
            device_id_type=MESH,
        )

    def arrival(sweep, side):
        return pltpu.make_async_remote_copy(
            src_ref=got.at[sweep, side],
            dst_ref=got.at[sweep, side],
            send_sem=send_sem.at[sweep, side],
            recv_sem=recv_sem.at[sweep, side],
            device_id=sides[side][1],
            device_id_type=MESH,
        )

    def send(sweep, side):
        @pl.when(sides[side][0])
        def _():
            copy_to(sweep, side).start()

    out_ref[...] = first_ref[...]
    for sweep in range(ITERS - 1):
        coeffs = out_ref[...].astype(BF16)
        own[sweep] = coeffs
        for_east[sweep] = dot_t(east_ref[...], coeffs).astype(BF16)
        send(sweep, 0)
        send(sweep, 1)
        for_south[sweep] = dot_t(south_ref[...], coeffs).astype(BF16)
        send(sweep, 2)
        send(sweep, 3)
        total[...] = jnp.zeros_like(total)
        for side in (1, 3, 0, 2):
            @pl.when(sides[side][0])
            def _():
                arrival(sweep, side).wait_recv()
                value = got[sweep, side]
                if side == 2:
                    total[...] += dot(east_ref[...], value)
                elif side == 3:
                    total[...] += dot(south_ref[...], value)
                else:
                    total[...] += value.astype(F32)

        out_ref[...] = (
            (1.0 - damping) * out_ref[...]
            + first_ref[...]
            - damping * dot(inv_ref[...], total[...].astype(BF16))
        )
    for sweep in range(ITERS - 1):
        for side in range(4):
            @pl.when(sides[side][0])
            def _():
                copy_to(sweep, side).wait_send()


def sweeps_of(n_sx, n_sy, inverse, first, east, south):
    shape = first.shape
    further = ITERS - 1
    return pl.pallas_call(
        functools.partial(sweep_kernel, n_sx, n_sy),
        out_shape=jax.ShapeDtypeStruct(shape, F32),
        in_specs=[VMEM] * 4,
        out_specs=VMEM,
        scratch_shapes=[
            pltpu.VMEM((further,) + shape, BF16),
            pltpu.VMEM((further,) + shape, BF16),
            pltpu.VMEM((further,) + shape, BF16),
            pltpu.VMEM((further, 4) + shape, BF16),
            pltpu.VMEM(shape, F32),
            pltpu.SemaphoreType.DMA((further, 4)),
            pltpu.SemaphoreType.DMA((further, 4)),
        ],
        compiler_params=pltpu.CompilerParams(collective_id=0, has_side_effects=True),
        name="sweeps",
    )(inverse, first, east, south)


def solution(mesh):
    n_sx, n_sy = mesh.shape["sx"], mesh.shape["sy"]

    def on_device(basis, diag_weight, correlation_weight, tile_ids, pair_live, loads, load_count):
        basis = basis[0, 0]
        ids = tile_ids[0, 0]
        row_at, col_at = lax.axis_index("sx"), lax.axis_index("sy")
        live = pair_live[row_at, col_at]
        live_east = jnp.logical_and(live[0] > 0, col_at < n_sy - 1)
        live_south = jnp.logical_and(live[1] > 0, row_at < n_sx - 1)
        lives = jnp.stack([live_east, live_south]).astype(F32)
        loads = loads[0, 0]
        count = (jnp.arange(loads.shape[1])[None, :] < load_count).astype(F32)
        a, x, size, inverse, first, block_east, block_south = assemble(
            n_sx, n_sy, ids, lives, count, basis, correlation_weight[0, 0], diag_weight[0, 0], loads
        )
        inverse, first = finish(count, size, a, x, loads, inverse, first)
        coeffs = sweeps_of(n_sx, n_sy, inverse, first, block_east, block_south)
        return coeffs[None, None]

    return jax.shard_map(
        on_device,
        mesh=mesh,
        in_specs=(
            P("sx", "sy", None, None),
            P("sx", "sy", None),
            P("sx", "sy", None, None),
            P("sx", "sy", None, None),
            P(),
            P("sx", "sy", None, None),
            P("sx", "sy"),
        ),
        out_specs=P("sx", "sy", None, None),
        check_vma=False,
    )
```

time: 106 us -> 95.1 us (0.90)
  waiting for transfers between devices: 20.3 us -> 0 us
  Pallas kernels: 73.6 us -> 87.5 us
  starting transfers between devices: 3.74 us -> 0 us
  local copies, waits for them, and re-layouts: 5.2 us -> 3.84 us
  other arithmetic: 0 us -> 1.2 us
    ppermute x2 -> x0, waiting for transfers between devices: 20.3 us -> none  [moved_back(): return lax.ppermute(block, axis, [(i + 1, i) for i in range(peers - 1)])]
    pallas_call x5 -> x2, Pallas kernels: 41.3 us -> 55.6 us  [the longest x1 54.8 us: assemble(): pl.pallas_call(functools.partial(assemble_kernel, n_sx, n_sy), out_shape=...]
    ppermute x2 -> x0, starting transfers between devices: 3.74 us -> none  [moved_back(): return lax.ppermute(block, axis, [(i + 1, i) for i in range(peers - 1)])]
    slice x2 -> x1, local copies, waits for them, and re-layouts: 1.94 us -> 0.55 us  [on_device(): live_east = jnp.logical_and(live[0] > 0, col_at < n_sy - 1)]
    convert_element_type x0 -> x2, other arithmetic: none -> 1.2 us  [the longest x1 0.62 us: on_device(): lives = jnp.stack([live_east, live_south]).astype(F32)]
    unnamed x5 -> x4, local copies, waits for them, and re-layouts: 3.18 us -> 3.21 us
  transfers between devices with their start and end apart: 2 -> 0, of which waited for: 1 -> 0; matrix products, arithmetic and copies ran while one was open for 1% -> 0% of each run, Pallas kernels for 29% -> 0%
where the time goes in v2:
time: 95.1 us; the launch traced here: 94.5 us
  Pallas kernels  87.5 us (92%)
  local copies, waits for them, and re-layouts  3.84 us (4%)
  between operations  1.94 us (2%)
  other arithmetic  1.2 us (1%)
    pallas_call x1, Pallas kernels, assemble(): pl.pallas_call(functools.partial(assemble_kernel, n_sx, n_sy), out_shape=...  54.8 us
    pallas_call x1, Pallas kernels, sweeps_of(): pl.pallas_call(functools.partial(sweep_kernel, n_sx, n_sy), out_shape=jax...  31.9 us
    unnamed x4, local copies, waits for them, and re-layouts  3.21 us

profile of v2, /device:TPU:10, one launch (start us, length us, event | category | flops | bytes accessed | tf_op | source)
XLA Modules:
  0.0 94.5 jit_solution(4671618961129665649)
XLA Ops:
  0.0 0.0 copy-start
  0.7 0.0 copy-done
  0.7 0.1 constant_dynamic-slice_fusion
  0.8 0.6 fusion
  2.6 0.6 add_convert_fusion.live_ref
  3.2 0.6 compare_convert_fusion.count_ref
  3.8 1.3 %copy.12 = f32[1,2,16,128]{3,2,1,0:T(8,128)} copy(f32[1,2,16,128]{3,1,2,0:T(2,128)} %bitcast.22) | data formatting | bytes 32768
  5.1 54.8 %assemble.1 = (f32[512,512]{1,0:T(8,128)}, f32[512,512]{1,0:T(8,128)}, f32[1,512]{1,0:T(1,128)}, bf16[512,512]{1,0:T(8,128)(2,1)}, f32[512,256]{1,0:T(8,128)}, /...) custom-call(s32[4,16]{1,0:T(4,128)} %bitcast.23, f32[2]{0:T(128)} %add_convert_fusion.live_ref, ...), custom_call_target="tpu_custom_call" | custom-call | tf_op jit(solution)/shard_map/assemble/pallas_call | solution.py:238
  59.8 0.9 finish.1
  60.7 31.9 %sweeps.1 = f32[512,256]{1,0:T(8,128)} custom-call(bf16[512,512]{1,0:T(8,128)(2,1)} %get-tuple-element.19.inv_ref, f32[512,256]{1,0:T(8,128)} %get-tuple-element.20.first_ref, bf16[512,512]{1,0:T(8,128)(2,1)} %get-tuple-element.21.east_ref, bf16[512,512]{1,0:T(8,128)(2,1)} %get-tuple-element.22.south_ref), custom_call_target="tpu_custom_call" | custom-call | tf_op jit(solution)/shard_map/sweeps/pallas_call | solution.py:402
  92.6 1.9 %copy.17 = f32[1,1,512,256]{3,2,1,0:T(8,128)} copy(f32[1,1,512,256]{3,2,1,0:T(8,128)} %bitcast.17) | data formatting | bytes 1048576
Async XLA Ops:
  0.0 0.7 copy-start

commit v3 on v2

--- a/solution.py
+++ b/solution.py
@@ -74,7 +74,8 @@
 
 
 def first_coeffs(split_a, inverse, loads, carried):
-    rhs = loads * carried
+    column = lax.broadcasted_iota(jnp.int32, loads.shape, 1)
+    rhs = loads * jnp.clip(carried - column, 0, 1).astype(F32)
     y = dot(inverse, rhs.astype(BF16))
     y = y + dot(inverse, (rhs - dot3(split_a, split(y))).astype(BF16))
     return damping * y
@@ -103,18 +104,32 @@
 
 
 def assemble_kernel(
-    n_sx, n_sy, ids_ref, live_ref, count_ref, basis_ref, corr_ref, weight_ref, loads_ref,
+    n_sx, n_sy, ids_ref, live_ref, count_ref, basis_hbm, corr_ref, weight_ref, loads_ref,
     a_out, x_out, size_ref, inv_ref, first_ref, east_ref, south_ref,
-    a_ref, x_ref, block_ref, sent, got, send_sem, recv_sem, local_sem,
+    basis_ref, a_ref, x_ref, block_ref, sent, got, send_sem, recv_sem, local_sem,
 ):
     rows, width = basis_ref.shape[0] * TILE, basis_ref.shape[2]
     half = width // 2
-    tiles = corr_ref.shape[1]
+    tiles = corr_ref.shape[1] // TILE
     per = 2 if tiles % 2 == 0 else 1
     chunk = per * TILE
     chunks = tiles // per
     sides = neighbours(n_sx, n_sy)
+    parts = 4
+    share = basis_ref.shape[0] // parts
+    loading = [
+        pltpu.make_async_copy(
+            basis_hbm.at[pl.ds(k * share, share)],
+            basis_ref.at[pl.ds(k * share, share)],
+            local_sem.at[2 + k],
+        )
+        for k in range(parts)
+    ]
+    for copy in loading:
+        copy.start()
     meet(sides)
+    for copy in loading:
+        copy.wait()
 
     def piece(which, q, peer):
         at = pl.ds(pl.multiple_of(q * chunk, chunk), chunk)
@@ -137,7 +152,7 @@
                     t = q * per + k
                     at = pl.ds(pl.multiple_of(t * TILE, TILE), TILE)
                     sent[which, at, :] = image_tile(
-                        basis_ref, ids_ref, 2 * which, t, tiles, corr_ref[which, pl.ds(t, 1), :]
+                        basis_ref, ids_ref, 2 * which, t, tiles, corr_ref[which : which + 1, at]
                     )
                 piece(which, q, which).start()
 
@@ -194,7 +209,7 @@
     x_copy.start()
     inverse = x_ref[...].astype(BF16)
     inv_ref[...] = inverse
-    first_ref[...] = first_coeffs(split_a, inverse, loads_ref[...], count_ref[...])
+    first_ref[...] = first_coeffs(split_a, inverse, loads_ref[...], count_ref[0, 0])
 
     for which, out_ref in ((1, south_ref), (0, east_ref)):
         block_ref[...] = jnp.zeros_like(block_ref)
@@ -214,7 +229,9 @@
                 )
                 block_ref[...] += dot_t(mine, got[which, at, :])
 
-        out_ref[...] = (block_ref[...] * live_ref[which]).astype(BF16)
+        out_ref[...] = (
+            block_ref[...] * live_ref[lax.axis_index("sx"), lax.axis_index("sy"), which].astype(F32)
+        ).astype(BF16)
 
     for which in range(2):
 
@@ -241,9 +258,10 @@
             square, square, jax.ShapeDtypeStruct((1, width), F32), short,
             jax.ShapeDtypeStruct(loads.shape, F32), short, short,
         ),
-        in_specs=[SMEM, SMEM, VMEM, VMEM, VMEM, VMEM, VMEM],
+        in_specs=[SMEM, SMEM, SMEM, ANY, VMEM, VMEM, VMEM],
         out_specs=(ANY, ANY, VMEM, VMEM, VMEM, VMEM, VMEM),
         scratch_shapes=[
+            pltpu.VMEM((rows // TILE, TILE, width), BF16),
             pltpu.VMEM((width, width), F32),
             pltpu.VMEM((width, width), F32),
             pltpu.VMEM((width, width), F32),
@@ -251,12 +269,12 @@
             pltpu.VMEM((2, overlap, width), BF16),
             pltpu.SemaphoreType.DMA((2, chunks)),
             pltpu.SemaphoreType.DMA((2, chunks)),
-            pltpu.SemaphoreType.DMA((2,)),
+            pltpu.SemaphoreType.DMA((6,)),
         ],
         compiler_params=pltpu.CompilerParams(collective_id=1, has_side_effects=True),
         name="assemble",
     )(
-        ids, live, count, basis.reshape(rows // TILE, TILE, width), corr.reshape(2, tiles, TILE),
+        ids, live, count, basis.reshape(rows // TILE, TILE, width), corr,
         weight.reshape(rows // TILE, TILE), loads,
     )
 
@@ -299,7 +317,7 @@
         )
         inverse = x_ref[...].astype(BF16)
         inv_ref[...] = inverse
-        first_ref[...] = first_coeffs(split_a, inverse, loads_ref[...], count_ref[...])
+        first_ref[...] = first_coeffs(split_a, inverse, loads_ref[...], count_ref[0, 0])
         outputs = [
             pltpu.make_async_copy(inv_ref, inv_out, sems.at[3]),
             pltpu.make_async_copy(first_ref, first_out, sems.at[4]),
@@ -317,7 +335,7 @@
         out_shape=(
             jax.ShapeDtypeStruct(inverse.shape, BF16), jax.ShapeDtypeStruct(first.shape, F32),
         ),
-        in_specs=[VMEM, VMEM, ANY, ANY, ANY, ANY, ANY],
+        in_specs=[SMEM, VMEM, ANY, ANY, ANY, ANY, ANY],
         out_specs=(ANY, ANY),
         scratch_shapes=[
             square, square, pltpu.VMEM(loads.shape, F32), pltpu.VMEM(inverse.shape, BF16),
@@ -335,48 +353,51 @@
     sides = neighbours(n_sx, n_sy)
     meet(sides)
 
-    def copy_to(sweep, side):
+    halves, span = own.shape[1], own.shape[3]
+
+    def copy_to(sweep, part, side):
         source = (own, own, for_east, for_south)[side]
         return pltpu.make_async_remote_copy(
-            src_ref=source.at[sweep],
-            dst_ref=got.at[sweep, (side + 2) % 4],
-            send_sem=send_sem.at[sweep, side],
-            recv_sem=recv_sem.at[sweep, (side + 2) % 4],
+            src_ref=source.at[sweep, part],
+            dst_ref=got.at[sweep, part, (side + 2) % 4],
+            send_sem=send_sem.at[sweep, part, side],
+            recv_sem=recv_sem.at[sweep, part, (side + 2) % 4],
             device_id=sides[side][1],
             device_id_type=MESH,
         )
 
-    def arrival(sweep, side):
+    def arrival(sweep, part, side):
+        place = got.at[sweep, part, side]
         return pltpu.make_async_remote_copy(
-            src_ref=got.at[sweep, side],
-            dst_ref=got.at[sweep, side],
-            send_sem=send_sem.at[sweep, side],
-            recv_sem=recv_sem.at[sweep, side],
+            src_ref=place,
+            dst_ref=place,
+            send_sem=send_sem.at[sweep, part, side],
+            recv_sem=recv_sem.at[sweep, part, side],
             device_id=sides[side][1],
             device_id_type=MESH,
         )
 
-    def send(sweep, side):
+    def send(sweep, part, side):
         @pl.when(sides[side][0])
         def _():
-            copy_to(sweep, side).start()
-
-    out_ref[...] = first_ref[...]
-    for sweep in range(ITERS - 1):
-        coeffs = out_ref[...].astype(BF16)
-        own[sweep] = coeffs
-        for_east[sweep] = dot_t(east_ref[...], coeffs).astype(BF16)
-        send(sweep, 0)
-        send(sweep, 1)
-        for_south[sweep] = dot_t(south_ref[...], coeffs).astype(BF16)
-        send(sweep, 2)
-        send(sweep, 3)
+            copy_to(sweep, part, side).start()
+
+    def give(sweep, part, coeffs):
+        own[sweep, part] = coeffs
+        for_east[sweep, part] = dot_t(east_ref[...], coeffs).astype(BF16)
+        send(sweep, part, 0)
+        send(sweep, part, 1)
+        for_south[sweep, part] = dot_t(south_ref[...], coeffs).astype(BF16)
+        send(sweep, part, 2)
+        send(sweep, part, 3)
+
+    def take(sweep, part, coeffs, initial):
         total[...] = jnp.zeros_like(total)
         for side in (1, 3, 0, 2):
             @pl.when(sides[side][0])
             def _():
-                arrival(sweep, side).wait_recv()
-                value = got[sweep, side]
+                arrival(sweep, part, side).wait_recv()
+                value = got[sweep, part, side]
                 if side == 2:
                     total[...] += dot(east_ref[...], value)
                 elif side == 3:
@@ -384,34 +405,45 @@
                 else:
                     total[...] += value.astype(F32)
 
-        out_ref[...] = (
-            (1.0 - damping) * out_ref[...]
-            + first_ref[...]
-            - damping * dot(inv_ref[...], total[...].astype(BF16))
-        )
+        moved = dot(inv_ref[...], total[...].astype(BF16))
+        return (1.0 - damping) * coeffs + initial - damping * moved
+
+    for part in range(halves):
+        give(0, part, first_ref[:, part * span : (part + 1) * span].astype(BF16))
     for sweep in range(ITERS - 1):
-        for side in range(4):
-            @pl.when(sides[side][0])
-            def _():
-                copy_to(sweep, side).wait_send()
+        for part in range(halves):
+            at = slice(part * span, (part + 1) * span)
+            before = first_ref[:, at] if sweep == 0 else out_ref[:, at]
+            coeffs = take(sweep, part, before, first_ref[:, at])
+            out_ref[:, at] = coeffs
+            if sweep < ITERS - 2:
+                give(sweep + 1, part, coeffs.astype(BF16))
+    for sweep in range(ITERS - 1):
+        for part in range(halves):
+            for side in range(4):
+                @pl.when(sides[side][0])
+                def _():
+                    copy_to(sweep, part, side).wait_send()
 
 
 def sweeps_of(n_sx, n_sy, inverse, first, east, south):
     shape = first.shape
     further = ITERS - 1
+    halves = 2 if shape[1] % (2 * TILE) == 0 else 1
+    piece = (shape[0], shape[1] // halves)
     return pl.pallas_call(
         functools.partial(sweep_kernel, n_sx, n_sy),
         out_shape=jax.ShapeDtypeStruct(shape, F32),
         in_specs=[VMEM] * 4,
         out_specs=VMEM,
         scratch_shapes=[
-            pltpu.VMEM((further,) + shape, BF16),
-            pltpu.VMEM((further,) + shape, BF16),
-            pltpu.VMEM((further,) + shape, BF16),
-            pltpu.VMEM((further, 4) + shape, BF16),
-            pltpu.VMEM(shape, F32),
-            pltpu.SemaphoreType.DMA((further, 4)),
-            pltpu.SemaphoreType.DMA((further, 4)),
+            pltpu.VMEM((further, halves) + piece, BF16),
+            pltpu.VMEM((further, halves) + piece, BF16),
+            pltpu.VMEM((further, halves) + piece, BF16),
+            pltpu.VMEM((further, halves, 4) + piece, BF16),
+            pltpu.VMEM(piece, F32),
+            pltpu.SemaphoreType.DMA((further, halves, 4)),
+            pltpu.SemaphoreType.DMA((further, halves, 4)),
         ],
         compiler_params=pltpu.CompilerParams(collective_id=0, has_side_effects=True),
         name="sweeps",
@@ -424,17 +456,11 @@
     def on_device(basis, diag_weight, correlation_weight, tile_ids, pair_live, loads, load_count):
         basis = basis[0, 0]
         ids = tile_ids[0, 0]
-        row_at, col_at = lax.axis_index("sx"), lax.axis_index("sy")
-        live = pair_live[row_at, col_at]
-        live_east = jnp.logical_and(live[0] > 0, col_at < n_sy - 1)
-        live_south = jnp.logical_and(live[1] > 0, row_at < n_sx - 1)
-        lives = jnp.stack([live_east, live_south]).astype(F32)
         loads = loads[0, 0]
-        count = (jnp.arange(loads.shape[1])[None, :] < load_count).astype(F32)
         a, x, size, inverse, first, block_east, block_south = assemble(
-            n_sx, n_sy, ids, lives, count, basis, correlation_weight[0, 0], diag_weight[0, 0], loads
-        )
-        inverse, first = finish(count, size, a, x, loads, inverse, first)
+            n_sx, n_sy, ids, pair_live, load_count, basis, correlation_weight[0, 0], diag_weight[0, 0], loads
+        )
+        inverse, first = finish(load_count, size, a, x, loads, inverse, first)
         coeffs = sweeps_of(n_sx, n_sy, inverse, first, block_east, block_south)
         return coeffs[None, None]
 

time: 95.1 us -> 90.3 us (0.950)
  Pallas kernels: 87.5 us -> 86.1 us
  between operations: 1.94 us -> 0.68 us
  other arithmetic: 1.2 us -> 0 us
    convert_element_type x2 -> x0, other arithmetic: 1.2 us -> none  [the longest x1 0.62 us: on_device(): lives = jnp.stack([live_east, live_south]).astype(F32)]
    unnamed x4 -> x2, local copies, waits for them, and re-layouts: 3.21 us -> 3.25 us
where the time goes in v3:
time: 90.3 us; the launch traced here: 90 us
  Pallas kernels  86.1 us (95%)
  local copies, waits for them, and re-layouts  3.25 us (4%)
    pallas_call x1, Pallas kernels, assemble(): pl.pallas_call(functools.partial(assemble_kernel, n_sx, n_sy), out_shape=...  54 us
    pallas_call x1, Pallas kernels, sweeps_of(): pl.pallas_call(functools.partial(sweep_kernel, n_sx, n_sy), out_shape=jax...  31.2 us
    unnamed x2, local copies, waits for them, and re-layouts  3.25 us

profile of v3, /device:TPU:10, one launch (start us, length us, event | category | flops | bytes accessed | tf_op | source)
XLA Modules:
  0.0 90.0 jit_solution(10316907699209665090)
XLA Ops:
  0.7 1.4 %copy.10.live_ref = s32[4,8,2]{2,1,0:T(8,128)} copy(s32[4,8,2]{1,2,0:T(2,128)} %param.11) | data formatting | bytes 512 | tf_op args[4]
  2.0 54.0 %assemble.1 = (f32[512,512]{1,0:T(8,128)}, f32[512,512]{1,0:T(8,128)}, f32[1,512]{1,0:T(1,128)}, bf16[512,512]{1,0:T(8,128)(2,1)}, f32[512,256]{1,0:T(8,128)}, /...) custom-call(s32[4,16]{1,0:T(4,128)} %bitcast.12, s32[4,8,2]{2,1,0:T(8,128)} %copy.10.live_ref, ...), custom_call_target="tpu_custom_call" | custom-call | tf_op jit(solution)/shard_map/assemble/pallas_call | solution.py:255
  56.1 0.8 finish.1
  56.9 31.2 %sweeps.1 = f32[512,256]{1,0:T(8,128)} custom-call(bf16[512,512]{1,0:T(8,128)(2,1)} %get-tuple-element.19.inv_ref, f32[512,256]{1,0:T(8,128)} %get-tuple-element.20.first_ref, bf16[512,512]{1,0:T(8,128)(2,1)} %get-tuple-element.21.east_ref, bf16[512,512]{1,0:T(8,128)(2,1)} %get-tuple-element.22.south_ref), custom_call_target="tpu_custom_call" | custom-call | tf_op jit(solution)/shard_map/sweeps/pallas_call | solution.py:434
  88.2 1.9 %copy.15 = f32[1,1,512,256]{3,2,1,0:T(8,128)} copy(f32[1,1,512,256]{3,2,1,0:T(8,128)} %bitcast.9) | data formatting | bytes 1048576

commit v4 on v3

--- a/solution.py
+++ b/solution.py
@@ -227,11 +227,13 @@
                     ],
                     axis=0,
                 )
-                block_ref[...] += dot_t(mine, got[which, at, :])
-
-        out_ref[...] = (
-            block_ref[...] * live_ref[lax.axis_index("sx"), lax.axis_index("sy"), which].astype(F32)
-        ).astype(BF16)
+                there = got[which, at, :]
+                block_ref[0] += dot_t(mine, there)
+                block_ref[1] += dot_t(there, mine)
+
+        live = live_ref[lax.axis_index("sx"), which, lax.axis_index("sy")].astype(F32)
+        for k in range(2):
+            out_ref[k] = (block_ref[k] * live).astype(BF16)
 
     for which in range(2):
 
@@ -252,11 +254,12 @@
     chunks = tiles // 2 if tiles % 2 == 0 else tiles
     square = jax.ShapeDtypeStruct((width, width), F32)
     short = jax.ShapeDtypeStruct((width, width), BF16)
+    pair = jax.ShapeDtypeStruct((2, width, width), BF16)
     return pl.pallas_call(
         functools.partial(assemble_kernel, n_sx, n_sy),
         out_shape=(
             square, square, jax.ShapeDtypeStruct((1, width), F32), short,
-            jax.ShapeDtypeStruct(loads.shape, F32), short, short,
+            jax.ShapeDtypeStruct(loads.shape, F32), pair, pair,
         ),
         in_specs=[SMEM, SMEM, SMEM, ANY, VMEM, VMEM, VMEM],
         out_specs=(ANY, ANY, VMEM, VMEM, VMEM, VMEM, VMEM),
@@ -264,7 +267,7 @@
             pltpu.VMEM((rows // TILE, TILE, width), BF16),
             pltpu.VMEM((width, width), F32),
             pltpu.VMEM((width, width), F32),
-            pltpu.VMEM((width, width), F32),
+            pltpu.VMEM((2, width, width), F32),
             pltpu.VMEM((2, overlap, width), BF16),
             pltpu.VMEM((2, overlap, width), BF16),
             pltpu.SemaphoreType.DMA((2, chunks)),
@@ -347,7 +350,7 @@
 
 
 def sweep_kernel(
-    n_sx, n_sy, inv_ref, first_ref, east_ref, south_ref, out_ref, own, for_east, for_south,
+    n_sx, n_sy, inv_ref, first_ref, east_ref, south_ref, out_ref, rest_ref, own, for_east, for_south,
     got, total, send_sem, recv_sem,
 ):
     sides = neighbours(n_sx, n_sy)
@@ -382,16 +385,18 @@
         def _():
             copy_to(sweep, part, side).start()
 
-    def give(sweep, part, coeffs):
+    def give_own(sweep, part, coeffs):
         own[sweep, part] = coeffs
-        for_east[sweep, part] = dot_t(east_ref[...], coeffs).astype(BF16)
         send(sweep, part, 0)
         send(sweep, part, 1)
-        for_south[sweep, part] = dot_t(south_ref[...], coeffs).astype(BF16)
+
+    def give_products(sweep, part, coeffs):
+        for_east[sweep, part] = dot(east_ref[1], coeffs).astype(BF16)
+        for_south[sweep, part] = dot(south_ref[1], coeffs).astype(BF16)
         send(sweep, part, 2)
         send(sweep, part, 3)
 
-    def take(sweep, part, coeffs, initial):
+    def take(sweep, part):
         total[...] = jnp.zeros_like(total)
         for side in (1, 3, 0, 2):
             @pl.when(sides[side][0])
@@ -399,31 +404,50 @@
                 arrival(sweep, part, side).wait_recv()
                 value = got[sweep, part, side]
                 if side == 2:
-                    total[...] += dot(east_ref[...], value)
+                    total[...] += dot(east_ref[0], value)
                 elif side == 3:
-                    total[...] += dot(south_ref[...], value)
+                    total[...] += dot(south_ref[0], value)
                 else:
                     total[...] += value.astype(F32)
 
-        moved = dot(inv_ref[...], total[...].astype(BF16))
-        return (1.0 - damping) * coeffs + initial - damping * moved
-
+    spans = [slice(part * span, (part + 1) * span) for part in range(halves)]
+    coeffs = [first_ref[:, at].astype(BF16) for at in spans]
     for part in range(halves):
-        give(0, part, first_ref[:, part * span : (part + 1) * span].astype(BF16))
+        give_own(0, part, coeffs[part])
+    for part in range(halves):
+        give_products(0, part, coeffs[part])
+    out_ref[...] = (2.0 - damping) * first_ref[...]
     for sweep in range(ITERS - 1):
-        for part in range(halves):
-            at = slice(part * span, (part + 1) * span)
-            before = first_ref[:, at] if sweep == 0 else out_ref[:, at]
-            coeffs = take(sweep, part, before, first_ref[:, at])
-            out_ref[:, at] = coeffs
-            if sweep < ITERS - 2:
-                give(sweep + 1, part, coeffs.astype(BF16))
+        for part, at in enumerate(spans):
+            take(sweep, part)
+            if sweep == ITERS - 2:
+                rest_ref[:, at] = total[...].astype(BF16)
+                continue
+            moved = out_ref[:, at] - damping * dot(inv_ref[...], total[...].astype(BF16))
+            coeffs = moved.astype(BF16)
+            give_own(sweep + 1, part, coeffs)
+            give_products(sweep + 1, part, coeffs)
+            out_ref[:, at] = (1.0 - damping) * moved + first_ref[:, at]
     for sweep in range(ITERS - 1):
         for part in range(halves):
             for side in range(4):
                 @pl.when(sides[side][0])
                 def _():
                     copy_to(sweep, part, side).wait_send()
+
+
+def settle_kernel(inv_ref, part_ref, rest_ref, out_ref):
+    out_ref[...] = part_ref[...] - damping * dot(inv_ref[...], rest_ref[...])
+
+
+def settle(inverse, part, rest):
+    return pl.pallas_call(
+        settle_kernel,
+        out_shape=jax.ShapeDtypeStruct(part.shape, F32),
+        in_specs=[VMEM] * 3,
+        out_specs=VMEM,
+        name="settle",
+    )(inverse, part, rest)
 
 
 def sweeps_of(n_sx, n_sy, inverse, first, east, south):
@@ -433,9 +457,9 @@
     piece = (shape[0], shape[1] // halves)
     return pl.pallas_call(
         functools.partial(sweep_kernel, n_sx, n_sy),
-        out_shape=jax.ShapeDtypeStruct(shape, F32),
+        out_shape=(jax.ShapeDtypeStruct(shape, F32), jax.ShapeDtypeStruct(shape, BF16)),
         in_specs=[VMEM] * 4,
-        out_specs=VMEM,
+        out_specs=(VMEM, VMEM),
         scratch_shapes=[
             pltpu.VMEM((further, halves) + piece, BF16),
             pltpu.VMEM((further, halves) + piece, BF16),
@@ -458,10 +482,11 @@
         ids = tile_ids[0, 0]
         loads = loads[0, 0]
         a, x, size, inverse, first, block_east, block_south = assemble(
-            n_sx, n_sy, ids, pair_live, load_count, basis, correlation_weight[0, 0], diag_weight[0, 0], loads
+            n_sx, n_sy, ids, pair_live.transpose(0, 2, 1), load_count, basis, correlation_weight[0, 0], diag_weight[0, 0], loads
         )
         inverse, first = finish(load_count, size, a, x, loads, inverse, first)
-        coeffs = sweeps_of(n_sx, n_sy, inverse, first, block_east, block_south)
+        part, rest = sweeps_of(n_sx, n_sy, inverse, first, block_east, block_south)
+        coeffs = settle(inverse, part, rest)
         return coeffs[None, None]
 
     return jax.shard_map(

time: 90.3 us -> 89.3 us (0.989)
  local copies, waits for them, and re-layouts: 3.25 us -> 0 us
  Pallas kernels: 86.1 us -> 88.4 us
    unnamed x2 -> x0, local copies, waits for them, and re-layouts: 3.25 us -> none
    pallas_call x1 -> x2, Pallas kernels: 31.2 us -> 33 us  [the longest x1 30.6 us: sweeps_of(): pl.pallas_call(functools.partial(sweep_kernel, n_sx, n_sy), out_shape=(ja...]
where the time goes in v4:
time: 89.3 us; the launch traced here: 89.1 us
  Pallas kernels  88.4 us (99%)
    pallas_call x1, Pallas kernels, assemble(): pl.pallas_call(functools.partial(assemble_kernel, n_sx, n_sy), out_shape=...  54.6 us
    pallas_call x1, Pallas kernels, sweeps_of(): pl.pallas_call(functools.partial(sweep_kernel, n_sx, n_sy), out_shape=(ja...  30.6 us
    pallas_call x1, Pallas kernels, settle(): pl.pallas_call(settle_kernel, out_shape=jax.ShapeDtypeStruct(part.shape,...  2.35 us

profile of v4, /device:TPU:10, one launch (start us, length us, event | category | flops | bytes accessed | tf_op | source)
XLA Modules:
  0.0 89.1 jit_solution(8571359010902813290)
XLA Ops:
  0.7 54.6 %assemble.1 = (f32[512,512]{1,0:T(8,128)}, f32[512,512]{1,0:T(8,128)}, f32[1,512]{1,0:T(1,128)}, bf16[512,512]{1,0:T(8,128)(2,1)}, f32[512,256]{1,0:T(8,128)}, /...) custom-call(s32[4,16]{1,0:T(4,128)} %bitcast.13, s32[4,2,8]{2,1,0:T(2,128)} %bitcast.12, ...), custom_call_target="tpu_custom_call" | custom-call | tf_op jit(solution)/shard_map/assemble/pallas_call | solution.py:258
  55.3 0.9 finish.1
  56.1 30.6 %sweeps.1 = (f32[512,256]{1,0:T(8,128)}, bf16[512,256]{1,0:T(8,128)(2,1)}) custom-call(bf16[512,512]{1,0:T(8,128)(2,1)} %get-tuple-element.21.inv_ref, f32[512,256]{1,0:T(8,128)} %get-tuple-element.22.first_ref, bf16[2,512,512]{2,1,0:T(8,128)(2,1)} %get-tuple-element.23.east_ref, bf16[2,512,512]{2,1,0:T(8,128)(2,1)} %get-tuple-element.24.south_ref), custom_call_target="tpu_custom_call" | custom-call | tf_op jit(solution)/shard_map/sweeps/pallas_call | solution.py:458
  86.8 2.4 %settle.1 = f32[512,256]{1,0:T(8,128)} custom-call(bf16[512,512]{1,0:T(8,128)(2,1)} %get-tuple-element.21.inv_ref, f32[512,256]{1,0:T(8,128)} %get-tuple-element.25.part_ref, bf16[512,256]{1,0:T(8,128)(2,1)} %get-tuple-element.26.rest_ref), custom_call_target="tpu_custom_call" | custom-call | tf_op jit(solution)/shard_map/settle/pallas_call | solution.py:444

commit v5 on v4

--- a/solution.py
+++ b/solution.py
@@ -350,10 +350,18 @@
 
 
 def sweep_kernel(
-    n_sx, n_sy, inv_ref, first_ref, east_ref, south_ref, out_ref, rest_ref, own, for_east, for_south,
+    n_sx, n_sy, inv_hbm, first_ref, east_hbm, south_hbm, out_ref, rest_ref, inv_ref, east_ref,
+    south_ref, local_sem, own, for_east, for_south,
     got, total, send_sem, recv_sem,
 ):
     sides = neighbours(n_sx, n_sy)
+    loading = [
+        pltpu.make_async_copy(east_hbm, east_ref, local_sem.at[0]),
+        pltpu.make_async_copy(south_hbm, south_ref, local_sem.at[1]),
+        pltpu.make_async_copy(inv_hbm, inv_ref, local_sem.at[2]),
+    ]
+    for copy in loading:
+        copy.start()
     meet(sides)
 
     halves, span = own.shape[1], own.shape[3]
@@ -414,6 +422,8 @@
     coeffs = [first_ref[:, at].astype(BF16) for at in spans]
     for part in range(halves):
         give_own(0, part, coeffs[part])
+    for copy in loading:
+        copy.wait()
     for part in range(halves):
         give_products(0, part, coeffs[part])
     out_ref[...] = (2.0 - damping) * first_ref[...]
@@ -458,9 +468,13 @@
     return pl.pallas_call(
         functools.partial(sweep_kernel, n_sx, n_sy),
         out_shape=(jax.ShapeDtypeStruct(shape, F32), jax.ShapeDtypeStruct(shape, BF16)),
-        in_specs=[VMEM] * 4,
+        in_specs=[ANY, VMEM, ANY, ANY],
         out_specs=(VMEM, VMEM),
         scratch_shapes=[
+            pltpu.VMEM(inverse.shape, BF16),
+            pltpu.VMEM(east.shape, BF16),
+            pltpu.VMEM(south.shape, BF16),
+            pltpu.SemaphoreType.DMA((3,)),
             pltpu.VMEM((further, halves) + piece, BF16),
             pltpu.VMEM((further, halves) + piece, BF16),
             pltpu.VMEM((further, halves) + piece, BF16),

time: 89.3 us -> 87.9 us (0.984)
  Pallas kernels: 88.4 us -> 86.9 us
    pallas_call x1, Pallas kernels: 30.6 us -> 29.1 us  [sweeps_of(): pl.pallas_call(functools.partial(sweep_kernel, n_sx, n_sy), out_shape=(ja...]
where the time goes in v5:
time: 87.9 us; the launch traced here: 87.6 us
  Pallas kernels  86.9 us (99%)
    pallas_call x1, Pallas kernels, assemble(): pl.pallas_call(functools.partial(assemble_kernel, n_sx, n_sy), out_shape=...  54.6 us
    pallas_call x1, Pallas kernels, sweeps_of(): pl.pallas_call(functools.partial(sweep_kernel, n_sx, n_sy), out_shape=(ja...  29.1 us
    pallas_call x1, Pallas kernels, settle(): pl.pallas_call(settle_kernel, out_shape=jax.ShapeDtypeStruct(part.shape,...  2.36 us

profile of v5, /device:TPU:10, one launch (start us, length us, event | category | flops | bytes accessed | tf_op | source)
XLA Modules:
  0.0 87.6 jit_solution(10539816901559820086)
XLA Ops:
  0.7 54.6 %assemble.1 = (f32[512,512]{1,0:T(8,128)}, f32[512,512]{1,0:T(8,128)}, f32[1,512]{1,0:T(1,128)}, bf16[512,512]{1,0:T(8,128)(2,1)}, f32[512,256]{1,0:T(8,128)}, /...) custom-call(s32[4,16]{1,0:T(4,128)} %bitcast.13, s32[4,2,8]{2,1,0:T(2,128)} %bitcast.12, ...), custom_call_target="tpu_custom_call" | custom-call | tf_op jit(solution)/shard_map/assemble/pallas_call | solution.py:258
  55.3 0.9 finish.1
  56.1 29.1 %sweeps.1 = (f32[512,256]{1,0:T(8,128)}, bf16[512,256]{1,0:T(8,128)(2,1)}) custom-call(bf16[512,512]{1,0:T(8,128)(2,1)} %get-tuple-element.21.inv_hbm.inv_ref, f32[512,256]{1,0:T(8,128)} %get-tuple-element.22.first_ref, bf16[2,512,512]{2,1,0:T(8,128)(2,1)} %get-tuple-element.23.east_hbm, bf16[2,512,512]{2,1,0:T(8,128)(2,1)} %get-tuple-element.24.south_hbm), custom_call_target="tpu_custom_call" | custom-call | tf_op jit(solution)/shard_map/sweeps/pallas_call | solution.py:468
  85.2 2.4 %settle.1 = f32[512,256]{1,0:T(8,128)} custom-call(bf16[512,512]{1,0:T(8,128)(2,1)} %get-tuple-element.21.inv_hbm.inv_ref, f32[512,256]{1,0:T(8,128)} %get-tuple-element.25.part_ref, bf16[512,256]{1,0:T(8,128)(2,1)} %get-tuple-element.26.rest_ref), custom_call_target="tpu_custom_call" | custom-call | tf_op jit(solution)/shard_map/settle/pallas_call | solution.py:454
